TPU v7x, 256 devices: a whole 4x4x8 slice. The times are simulated.
256 devices in a mesh: shot: 4 (over x), band: 32 (over y_lo, z, core), net: 2 (over y_hi).
Axes of the slice: x: 4, y: 4 (y_hi: 2, y_lo: 2; y = y_hi * 2 + y_lo), z: 8, core: 2. Of those that a mesh axis runs over, the one named last changes fastest.
Arguments:
- velocity: float32 [1024, 1024], P('band'), may hold values from 1.5 to 4
- wave_now: float32 [16, 1024, 1024], P(('shot', 'net'), 'band'), may hold values from -6 to 6
- wave_before: float32 [16, 1024, 1024], P(('shot', 'net'), 'band'), may hold values from -6 to 6
- adjoint_last: float32 [16, 1024, 1024], P(('shot', 'net'), 'band'), may hold values from -6 to 6
- adjoint_after: float32 [16, 1024, 1024], P(('shot', 'net'), 'band'), may hold values from -6 to 6
- wavelet: float32 [16, 16], P(('shot', 'net')), may hold values from -72 to 72
- source_col: int32 [16], P(('shot', 'net')), may hold values from 0 to 1023
- rec_first: int32 [16], P(('shot', 'net')), may hold values from 0 to 1022
- rec_last: int32 [16], P(('shot', 'net')), may hold values from 1 to 1023
- rec_count: int32 [16], P(('shot', 'net')), may hold values from 2 to 128, as said below
- observed: float32 [16, 16, 128], P(('shot', 'net')), may hold values from -72 to 72
- conv_in: float32 [32, 18], replicated, may hold values from -1.5 to 1.5
- conv_mid: float32 [32, 288], replicated, may hold values from -0.375 to 0.375
- conv_out: float32 [1, 288], replicated, may hold values from -0.375 to 0.375
- cotangent: float32 [1024, 1024], P('band', ('shot', 'net')), may hold values from -0.0234375 to 0.0234375
Outputs:
- new_velocity: float32 [1024, 1024], P('band', ('shot', 'net'))
- grad_in: float32 [32, 18], replicated
- grad_mid: float32 [32, 288], replicated
- grad_out: float32 [1, 288], replicated
Inputs may be any that keep to these rules, and one draw needn't show every extreme that they name: rec_last - rec_first >= rec_count - 1 for every shot; some shot has 128 receivers.
All inputs are finite; a program needn't handle non-finite values.
Results may differ from a plain program's by a relative error of at most 0.0003.
Values sent between devices are 32-bit elements; how exact they have to be, the bound alone decides.
No kernel may reach another device: no remote copies, remote signals or barrier semaphores. Data moves between devices by JAX's collectives and lax.ppermute only.
A program may use at most 128 MiB of HBM per device.

v0:
```python
import functools

import jax
import jax.numpy as jnp
from jax import lax
from jax.sharding import Mesh
from jax.sharding import PartitionSpec as P

BAND = ("band_0", "band_1", "band_2")
SHOT_BAND_NET = ("shot", "band_0", "band_1", "band_2", "net")


coefficients = (-205.0 / 72.0, 8.0 / 5.0, -1.0 / 5.0, 8.0 / 315.0, -1.0 / 560.0)
speed_factor = 0.11
source_depth = 2
receiver_depth = 3
highest = lax.Precision.HIGHEST


def extended_2(block, sides, width):
    for axis, dim in sides:
        count = lax.axis_size(axis)
        forward = [(i, i + 1) for i in range(count - 1)]
        backward = [(target, source) for source, target in forward]
        low = lax.ppermute(
            lax.slice_in_dim(block, block.shape[dim] - width, None, axis=dim), axis, forward
        )
        high = lax.ppermute(lax.slice_in_dim(block, 0, width, axis=dim), axis, backward)
        block = jnp.concatenate([low, block, high], axis=dim)
    return block


def copy_for_each(x, axis):
    peers = lax.axis_size(axis)
    return lax.all_to_all(jnp.broadcast_to(x[None], (peers, *x.shape)), axis, 0, 0, tiled=True)


def over_copies(x, axis):
    everything = copy_for_each(x, axis)
    return jnp.sum(everything, axis=0)


def by_axis(x, axes):
    return functools.reduce(lax.psum, axes, x)


def laplace(extended):
    middle = extended[..., 4:-4, :]
    height = middle.shape[-2]
    breadth = middle.shape[-1]
    padding = [(0, 0)] * (middle.ndim - 1) + [(4, 4)]
    padded = jnp.pad(middle, padding)
    running = 2.0 * coefficients[0] * middle
    for reach in range(1, 5):
        vertical = (
            extended[..., 4 - reach : 4 - reach + height, :]
            + extended[..., 4 + reach : 4 + reach + height, :]
        )
        lateral = (
            padded[..., 4 - reach : 4 - reach + breadth]
            + padded[..., 4 + reach : 4 + reach + breadth]
        )
        running = running + coefficients[reach] * (vertical + lateral)
    return running


def receiver_table(rec_first, rec_last, rec_count, breadth, slots):
    columns = jnp.arange(breadth, dtype=jnp.int32)
    slot_ids = jnp.arange(slots, dtype=jnp.int32)
    placed = (
        rec_first[:, None]
        + slot_ids[None, :] * (rec_last - rec_first)[:, None] // (rec_count - 1)[:, None]
    )
    active = slot_ids[None, :] < rec_count[:, None]
    return ((columns[None, :, None] == placed[:, None, :]) & active[:, None, :]).astype(jnp.float32)


def patches(extended, height, breadth):
    parts = [
        extended[:, down : down + height, across : across + breadth]
        for down in range(3)
        for across in range(3)
    ]
    return jnp.concatenate(parts, 0).reshape(-1, height * breadth)


def flipped(weights):
    outputs = weights.shape[0]
    channels = weights.shape[1] // 9
    return (
        weights.reshape(outputs, 9, channels)[:, ::-1, :]
        .transpose(2, 1, 0)
        .reshape(channels, 9 * outputs)
    )


def sigmoid_slope(values):
    squashed = jax.nn.sigmoid(values)
    return squashed * (1.0 + values * (1.0 - squashed))


def matmul(left, right):
    return jnp.dot(left, right, precision=highest)


def outer_sum(left, right):
    return lax.dot_general(left, right, (((1,), (1,)), ((), ())), precision=highest)


def on_device(
    velocity,
    wave_now,
    wave_before,
    adjoint_last,
    adjoint_after,
    wavelet,
    source_col,
    rec_first,
    rec_last,
    rec_count,
    observed,
    conv_in,
    conv_mid,
    conv_out,
    cotangent,
):
    rows_here = velocity.shape[0]
    breadth = velocity.shape[1]
    shot_here = wave_now.shape[0]
    num_steps = wavelet.shape[1]
    slots = observed.shape[2]
    piece_cols = cotangent.shape[1]
    first_row = lax.axis_index(BAND) * rows_here
    speed_sq = (velocity * speed_factor) ** 2
    columns = jnp.arange(breadth, dtype=jnp.int32)
    source_cols = (columns[None, :] == source_col[:, None]).astype(jnp.float32)[:, None, :]
    table = receiver_table(rec_first, rec_last, rec_count, breadth, slots)
    active = (jnp.arange(slots, dtype=jnp.int32)[None, :] < rec_count[:, None]).astype(jnp.float32)

    def source_term(row_start, height, amount):
        row_ids = row_start + jnp.arange(height, dtype=jnp.int32)
        marked = (row_ids == source_depth).astype(jnp.float32)[None, :, None]
        return marked * source_cols * amount[:, None, None]

    def receiver_term(row_start, height, residual):
        row_ids = row_start + jnp.arange(height, dtype=jnp.int32)
        marked = (row_ids == receiver_depth).astype(jnp.float32)[None, :, None]
        injected = jnp.einsum("swk,sk->sw", table, residual, precision=highest)
        return marked * injected[:, None, :]

    speed_wide = extended_2(speed_sq, ((BAND, 0),), 16)

    def propagate(start, prior, drive, inject):
        grouped = drive.reshape((num_steps // 4, 4) + drive.shape[1:])

        def block(carry, amounts):
            stacked = extended_2(jnp.stack([carry[0], carry[1]]), ((BAND, 2),), 16)
            current = stacked[0]
            earlier = stacked[1]
            margin = 16
            saved = []
            for offset in range(4):
                inner = margin - 4
                speed_part = speed_wide[16 - inner : 16 + rows_here + inner]
                fresh = (
                    2.0 * current[:, 4:-4]
                    - earlier[:, 4:-4]
                    + speed_part * laplace(current)
                    + inject(first_row - inner, rows_here + 2 * inner, amounts[offset])
                )
                earlier = current[:, 4:-4]
                current = fresh
                margin = inner
                saved.append(fresh[:, inner : inner + rows_here])
            return ((current, earlier), jnp.stack(saved))

        ignored, states = lax.scan(block, (start, prior), grouped)
        return states.reshape((num_steps,) + start.shape)

    stored = propagate(wave_now, wave_before, wavelet.T, source_term)
    samples = jnp.einsum("tsw,swk->tsk", stored[:, :, receiver_depth, :], table, precision=highest)
    misfit = (samples - jnp.transpose(observed, (1, 0, 2))) * active[None]
    adjoint = propagate(adjoint_last, adjoint_after, misfit[::-1], receiver_term)
    imaging = jnp.sum(stored * adjoint[::-1], axis=(0, 1))
    group_count = shot_here * lax.axis_size(("shot", "net"))
    start_col = lax.axis_index(("shot", "net")) * piece_cols
    gathered = over_copies(imaging, ("shot", "net"))
    summed = lax.dynamic_slice_in_dim(gathered, start_col, piece_cols, 1)
    scaled = summed / float(num_steps * group_count) ** 0.5
    velocity_piece = lax.dynamic_slice_in_dim(velocity, start_col, piece_cols, 1)

    def spread(field):
        extended = extended_2(field, ((BAND, 1), (("shot", "net"), 2)), 1)
        return patches(extended, rows_here, piece_cols)

    layer_zero = spread(jnp.stack([velocity_piece, scaled]))
    before_one = matmul(conv_in, layer_zero)
    hidden_one = jax.nn.silu(before_one)
    layer_one = spread(hidden_one.reshape(-1, rows_here, piece_cols))
    before_two = matmul(conv_mid, layer_one)
    hidden_two = jax.nn.silu(before_two)
    layer_two = spread(hidden_two.reshape(-1, rows_here, piece_cols))
    update = matmul(conv_out, layer_two).reshape(rows_here, piece_cols)
    new_velocity = velocity_piece + update
    grad_out = outer_sum(cotangent.reshape(1, -1), layer_two)
    slope_two = matmul(flipped(conv_out), spread(cotangent[None])) * sigmoid_slope(before_two)
    grad_mid = outer_sum(slope_two, layer_one)
    slope_one = matmul(
        flipped(conv_mid), spread(slope_two.reshape(-1, rows_here, piece_cols))
    ) * sigmoid_slope(before_one)
    grad_in = outer_sum(slope_one, layer_zero)
    totals = (
        by_axis(grad_in, SHOT_BAND_NET),
        by_axis(grad_mid, SHOT_BAND_NET),
        by_axis(grad_out, SHOT_BAND_NET),
    )
    return (new_velocity, totals[0], totals[1], totals[2])


def solution(mesh):
    split = Mesh(
        mesh.devices.reshape(mesh.shape["shot"], 2, 8, 2, mesh.shape["net"]),
        ("shot", "band_0", "band_1", "band_2", "net"),
    )
    placed = (
        P(BAND, None),
        P(("shot", "net"), BAND, None),
        P(("shot", "net"), BAND, None),
        P(("shot", "net"), BAND, None),
        P(("shot", "net"), BAND, None),
        P(("shot", "net"), None),
        P(("shot", "net")),
        P(("shot", "net")),
        P(("shot", "net")),
        P(("shot", "net")),
        P(("shot", "net"), None, None),
        P(),
        P(),
        P(),
        P(BAND, ("shot", "net")),
    )
    return jax.shard_map(
        on_device,
        mesh=split,
        in_specs=placed,
        out_specs=(P(BAND, ("shot", "net")), P(), P(), P()),
        check_vma=False,
    )
```

profile of v0, /device:TPU:32, one launch (start us, length us, event | category | flops | bytes accessed | tf_op | source)
XLA Modules:
  0.0 532.9 jit_solution(18065318332580031018)
XLA Ops:
  13.6 58.1 %while.34 = (s32[]{:T(128)}, f32[2,32,1024]{2,1,0:T(8,128)S(1)}, f32[2,32,1024]{2,1,0:T(8,128)S(1)}, f32[4,4,2,32,1024]{4,3,2,1,0:T(8,128)}, f32[64,1024]{1,0:T(...) while((s32[]{:T(128)}, f32[2,32,1024]{2,1,0:T(8,128)S(1)}, ...), condition=%wide.region_1.2_spmd.clone, body=%wide.region_0.1_spmd.clone.sunk | while | flops 11801106 | bytes 31434516 | solution.py:177
  19.4 3.8 collective-permute-done.1
  34.0 3.8 collective-permute-done.1
  48.5 3.8 collective-permute-done.1
  63.0 3.8 collective-permute-done.1
  71.7 4.6 copy.175
  79.4 59.5 %while.35 = (s32[]{:T(128)}, f32[2,32,1024]{2,1,0:T(8,128)S(1)}, f32[2,32,1024]{2,1,0:T(8,128)S(1)}, f32[4,4,2,32,1024]{4,3,2,1,0:T(8,128)}, f32[64,1024]{1,0:T(...) while((s32[]{:T(128)}, f32[2,32,1024]{2,1,0:T(8,128)S(1)}, ...), condition=%wide.region_3.4_spmd.clone, body=%wide.region_2.3_spmd.clone.sunk | while | flops 27165204 | bytes 31534800 | solution.py:177
  138.9 6.6 %copy.176 = f32[16,2,32,1024]{3,0,1,2:T(8,128)} copy(f32[16,2,32,1024]{3,2,1,0:T(8,128)} %bitcast.368) | data formatting | bytes 8388608 | tf_op jit(solution)/shard_map/reshape | solution.py:178
  145.5 7.2 %rev.13 = f32[16,2,32,1024]{3,0,1,2:T(8,128)} reverse(f32[16,2,32,1024]{3,0,1,2:T(8,128)} %copy.176), dimensions={0} | reverse | bytes 8388608 | tf_op jit(solution)/shard_map/rev | solution.py:184
  152.7 6.4 %multiply_reduce_fusion = f32[32,1024]{1,0:T(8,128)S(1)} fusion(f32[16,2,32,1024]{3,0,1,2:T(8,128)} %rev.13, f32[16,2,32,1024]{3,2,1,0:T(8,128)} %bitcast.367), kind=kLoop, calls=%fused_computation.332 | loop fusion | flops 2064384 | bytes 8519680 | tf_op jit(solution)/shard_map/reduce_sum | solution.py:184
  160.2 6.9 %all-to-all-start = ((f32[8,32,1024]{2,1,0:T(8,128)}), f32[8,32,1024]{2,1,0:T(8,128)S(1)}, u32[]{:S(2)}, u32[]{:S(2)}) async-start(f32[8,32,1024]{2,1,0:T(8,128)} %broadcast_in_dim.16), calls=%async_computation | async-start | bytes 2097152 | tf_op jit(solution)/shard_map/all_to_all | solution.py:35
  167.2 5.9 %collective-permute-start.18 = (f32[1,1,128]{2,1,0:T(1,128)S(1)}, f32[1,1,128]{2,1,0:T(1,128)S(1)}, u32[]{:S(2)}, u32[]{:S(2)}) collective-permute-start(f32[1,1,128]{2,1,0:T(1,128)S(1)} %get-tuple-element.603), channel_id=1, source_target_pairs={{0,2},{2,4},{4,6},{6,8},{8,10},{10,12},{12,14},{14,16},{16,18},{18... | collective-permute-start | bytes 1544 | tf_op jit(solution)/shard_map/ppermute | solution.py:25
  181.0 6.1 %collective-permute-start.20 = (f32[1,34,1]{2,1,0:T(8,128)S(1)}, f32[1,34,1]{2,1,0:T(8,128)S(1)}, u32[]{:S(2)}, u32[]{:S(2)}) collective-permute-start(f32[1,34,1]{2,1,0:T(8,128)S(1)} %get-tuple-element.598), channel_id=1, source_target_pairs={{0,1},{1,64},{64,65},{65,128},{128,129},{129,192},{192,193},{2,3},... | collective-permute-start | bytes 416 | tf_op jit(solution)/shard_map/ppermute | solution.py:25
  188.7 4.0 collective-permute-start.6
  194.7 4.3 collective-permute-done.7
  200.4 7.0 %collective-permute-start.8 = (f32[2,34,1]{2,1,0:T(8,128)S(1)}, f32[2,34,1]{2,1,0:T(8,128)S(1)}, u32[]{:S(2)}, u32[]{:S(2)}) collective-permute-start(f32[2,34,1]{2,1,0:T(8,128)S(1)} %get-tuple-element.590), channel_id=1, source_target_pairs={{0,1},{1,64},{64,65},{65,128},{128,129},{129,192},{192,193},{2,3},... | collective-permute-start | bytes 824 | tf_op jit(solution)/shard_map/ppermute | solution.py:25
  213.2 3.8 collective-permute-start.10
  229.4 7.1 %collective-permute-start.12 = (f32[32,34,1]{1,0,2:T(8,128)S(1)}, f32[32,34,1]{1,0,2:T(8,128)S(1)}, u32[]{:S(2)}, u32[]{:S(2)}) collective-permute-start(f32[32,34,1]{1,0,2:T(8,128)S(1)} %get-tuple-element.544), channel_id=1, source_target_pairs={{0,1},{1,64},{64,65},{65,128},{128,129},{129,192},{192,193},{2,3},... | collective-permute-start | bytes 13064 | tf_op jit(solution)/shard_map/ppermute | solution.py:25
  238.5 4.4 pad_maximum_fusion.4
  282.6 4.7 fusion.230
  290.8 5.5 %collective-permute-start.14 = (f32[32,1,128]{2,0,1:T(8,128)}, f32[32,1,128]{2,0,1:T(8,128)}, u32[]{:S(2)}, u32[]{:S(2)}) collective-permute-start(f32[32,1,128]{2,0,1:T(8,128)} %bitcast.94), channel_id=1, source_target_pairs={{0,2},{2,4},{4,6},{6,8},{8,10},{10,12},{12,14},{14,16},{16,18},{18... | collective-permute-start | bytes 49160 | tf_op jit(solution)/shard_map/ppermute | solution.py:25
  304.5 4.4 collective-permute-start.22
  318.3 7.6 %collective-permute-start.16 = (f32[32,34,1]{1,0,2:T(8,128)}, f32[32,34,1]{1,0,2:T(8,128)}, u32[]{:S(2)}, u32[]{:S(2)}) collective-permute-start(f32[32,34,1]{1,0,2:T(8,128)} %get-tuple-element.540), channel_id=1, source_target_pairs={{0,1},{1,64},{64,65},{65,128},{128,129},{129,192},{192,193},{2,3},... | collective-permute-start | bytes 13064 | tf_op jit(solution)/shard_map/ppermute | solution.py:25
  335.6 6.5 %collective-permute-start.24 = (f32[32,34,1]{1,0,2:T(8,128)S(1)}, f32[32,34,1]{1,0,2:T(8,128)S(1)}, u32[]{:S(2)}, u32[]{:S(2)}) collective-permute-start(f32[32,34,1]{1,0,2:T(8,128)S(1)} %get-tuple-element.536), channel_id=1, source_target_pairs={{0,1},{1,64},{64,65},{65,128},{128,129},{129,192},{192,193},{2,3},... | collective-permute-start | bytes 13064 | tf_op jit(solution)/shard_map/ppermute | solution.py:25
  361.7 7.2 %pad_maximum_fusion.5 = (f32[32,34,129]{1,0,2:T(8,128)S(1)}, f32[32,34,129]{1,0,2:T(8,128)S(1)}) fusion(f32[32,34,1]{1,0,2:T(8,128)} %collective-permute-done.17, f32[32,1,128]{1,0,2:T(8,128)} %copy.140, f32[32,32,128]{1,0,2:T(8,128)} %copy-done.6, f32[32,1,128]{1,0,2:T(8,128)} %copy.138, f32[32,34,1]{1,0,2:T(8,128)} %collective-permute-done.16), kind=kLoop, calls=%fused_computation.336 | loop fusion | flops 842112 | bytes 1688576 | tf_op jit(solution)/shard_map/concatenate | solution.py:29
  368.9 4.0 fusion.216
  383.4 6.8 %fusion.215 = (f32[32,32,128]{1,0,2:T(8,128)}, f32[32,32,128]{1,0,2:T(8,128)}, f32[32,32,128]{1,0,2:T(8,128)}) fusion(f32[32,34,129]{1,0,2:T(8,128)} %get-tuple-element.534), kind=kLoop, calls=%fused_computation.439 | loop fusion | bytes 3145728 | tf_op jit(solution)/shard_map/slice | solution.py:80
  434.2 4.0 fusion.231
  439.5 22.6 %all-reduce.9 = (f32[32,18]{0,1:T(8,128)S(1)}, f32[32,288]{1,0:T(8,128)S(1)}, f32[1,288]{1,0:T(1,128)S(1)}) all-reduce(f32[32,18]{0,1:T(8,128)S(1)} %copy-done.40, f32[32,288]{1,0:T(8,128)S(1)} %copy-done.39, f32[1,288]{1,0:T(1,128)S(1)} %fusion.231), channel_id=1, replica_groups=mesh['shot'=4,'band_0'=2,'band_1'=8,'band_2'=2,'net'=2] {'shot'}, use_global_device_ids=true, to_apply=%region_6.7 | all-reduce | flops 10080 | bytes 80640 | tf_op jit(solution)/shard_map/psum | solution.py:44
  462.1 24.9 %all-reduce.12 = (f32[32,18]{0,1:T(8,128)S(1)}, f32[32,288]{1,0:T(8,128)S(1)}, f32[1,288]{1,0:T(1,128)S(1)}) all-reduce(f32[32,18]{0,1:T(8,128)S(1)} %get-tuple-element.505, f32[32,288]{1,0:T(8,128)S(1)} %get-tuple-element.506, ...), channel_id=1, replica_groups=mesh['shot'=4,'band_0'=2,'band_1'=8,'band_2'=2,'net'=2] {'band_0'}, use_global_device_ids=true, to_apply=%region_7.8 | all-reduce | flops 10080 | bytes 80640 | tf_op jit(solution)/shard_map/psum | solution.py:44
  487.0 30.9 %all-reduce.8 = (f32[32,18]{0,1:T(8,128)S(1)}, f32[32,288]{1,0:T(8,128)S(1)}, f32[1,288]{1,0:T(1,128)S(1)}) all-reduce(f32[32,18]{0,1:T(8,128)S(1)} %get-tuple-element.514, f32[32,288]{1,0:T(8,128)S(1)} %get-tuple-element.515, ...), channel_id=1, replica_groups=mesh['shot'=4,'band_0'=2,'band_1'=8,'band_2'=2,'net'=2] {'band_1'}, use_global_device_ids=true, to_apply=%region_8.9 | all-reduce | flops 10080 | bytes 80640 | tf_op jit(solution)/shard_map/psum | solution.py:44
  521.4 11.3 %all-reduce.10 = (f32[32,18]{0,1:T(8,128)}, f32[32,288]{1,0:T(8,128)}, f32[1,288]{1,0:T(1,128)}) all-reduce(f32[32,18]{0,1:T(8,128)S(1)} %get-tuple-element.511, f32[32,288]{1,0:T(8,128)S(1)} %get-tuple-element.512, f32[1,288]{1,0:T(1,128)S(1)} %get-tuple-element.513), channel_id=1, replica_groups=mesh['shot'=4,'band_0'=2,'band_1'=8,'band_2'=2,'net'=2] {'net'}, use_global_device_ids=true, to_apply=%region_10.11 | all-reduce | flops 10080 | bytes 80640 | tf_op jit(solution)/shard_map/psum | solution.py:44
  (492 shorter events, 299.2 us)
Async XLA Ops:
  1.7 9.3 %collective-permute-start.4 = (f32[16,1024]{1,0:T(8,128)S(1)}, f32[16,1024]{1,0:T(8,128)S(1)}, u32[]{:S(2)}, u32[]{:S(2)}) collective-permute-start(f32[16,1024]{1,0:T(8,128)S(1)} %get-tuple-element.575), channel_id=1, source_target_pairs={{0,2},{2,4},{4,6},{6,8},{8,10},{10,12},{12,14},{14,16},{16,18},{18... | collective-permute-start | bytes 196616 | tf_op jit(solution)/shard_map/ppermute | solution.py:25
  3.6 7.3 %collective-permute-start.5 = (f32[16,1024]{1,0:T(8,128)S(1)}, f32[16,1024]{1,0:T(8,128)S(1)}, u32[]{:S(2)}, u32[]{:S(2)}) collective-permute-start(f32[16,1024]{1,0:T(8,128)S(1)} %get-tuple-element.576), channel_id=1, source_target_pairs={{2,0},{4,2},{6,4},{8,6},{10,8},{12,10},{14,12},{16,14},{18,16},{20... | collective-permute-start | bytes 196616 | tf_op jit(solution)/shard_map/ppermute | solution.py:28
  15.6 7.7 %collective-permute-start.1 = (f32[2,2,16,1024]{3,2,1,0:T(8,128)S(1)}, f32[2,2,16,1024]{3,2,1,0:T(8,128)S(1)}, u32[]{:S(2)}, u32[]{:S(2)}) collective-permute-start(f32[2,2,16,1024]{3,2,1,0:T(8,128)S(1)} %get-tuple-element.773), channel_id=1, source_target_pairs={{0,2},{2,4},{4,6},{6,8},{8,10},{10,12},{12,14},{14,16},{16,18},{18... | collective-permute-start | bytes 786440 | tf_op jit(solution)/shard_map/while/body/eval_jaxpr/ppermute | solution.py:25
  30.1 7.7 %collective-permute-start.1 = (f32[2,2,16,1024]{3,2,1,0:T(8,128)S(1)}, f32[2,2,16,1024]{3,2,1,0:T(8,128)S(1)}, u32[]{:S(2)}, u32[]{:S(2)}) collective-permute-start(f32[2,2,16,1024]{3,2,1,0:T(8,128)S(1)} %get-tuple-element.773), channel_id=1, source_target_pairs={{0,2},{2,4},{4,6},{6,8},{8,10},{10,12},{12,14},{14,16},{16,18},{18... | collective-permute-start | bytes 786440 | tf_op jit(solution)/shard_map/while/body/eval_jaxpr/ppermute | solution.py:25
  44.6 7.7 %collective-permute-start.1 = (f32[2,2,16,1024]{3,2,1,0:T(8,128)S(1)}, f32[2,2,16,1024]{3,2,1,0:T(8,128)S(1)}, u32[]{:S(2)}, u32[]{:S(2)}) collective-permute-start(f32[2,2,16,1024]{3,2,1,0:T(8,128)S(1)} %get-tuple-element.773), channel_id=1, source_target_pairs={{0,2},{2,4},{4,6},{6,8},{8,10},{10,12},{12,14},{14,16},{16,18},{18... | collective-permute-start | bytes 786440 | tf_op jit(solution)/shard_map/while/body/eval_jaxpr/ppermute | solution.py:25
  59.1 7.7 %collective-permute-start.1 = (f32[2,2,16,1024]{3,2,1,0:T(8,128)S(1)}, f32[2,2,16,1024]{3,2,1,0:T(8,128)S(1)}, u32[]{:S(2)}, u32[]{:S(2)}) collective-permute-start(f32[2,2,16,1024]{3,2,1,0:T(8,128)S(1)} %get-tuple-element.773), channel_id=1, source_target_pairs={{0,2},{2,4},{4,6},{6,8},{8,10},{10,12},{12,14},{14,16},{16,18},{18... | collective-permute-start | bytes 786440 | tf_op jit(solution)/shard_map/while/body/eval_jaxpr/ppermute | solution.py:25
  79.7 8.7 %collective-permute-start.2 = (f32[2,2,16,1024]{3,2,1,0:T(8,128)S(1)}, f32[2,2,16,1024]{3,2,1,0:T(8,128)S(1)}, u32[]{:S(2)}, u32[]{:S(2)}) collective-permute-start(f32[2,2,16,1024]{3,2,1,0:T(8,128)S(1)} %get-tuple-element.795), channel_id=1, source_target_pairs={{2,0},{4,2},{6,4},{8,6},{10,8},{12,10},{14,12},{16,14},{18,16},{20... | collective-permute-start | bytes 786440 | tf_op jit(solution)/shard_map/while/body/eval_jaxpr/ppermute | solution.py:28
  81.6 7.7 %collective-permute-start.3 = (f32[2,2,16,1024]{3,2,1,0:T(8,128)S(1)}, f32[2,2,16,1024]{3,2,1,0:T(8,128)S(1)}, u32[]{:S(2)}, u32[]{:S(2)}) collective-permute-start(f32[2,2,16,1024]{3,2,1,0:T(8,128)S(1)} %get-tuple-element.796), channel_id=1, source_target_pairs={{0,2},{2,4},{4,6},{6,8},{8,10},{10,12},{12,14},{14,16},{16,18},{18... | collective-permute-start | bytes 786440 | tf_op jit(solution)/shard_map/while/body/eval_jaxpr/ppermute | solution.py:25
  94.2 8.9 %collective-permute-start.2 = (f32[2,2,16,1024]{3,2,1,0:T(8,128)S(1)}, f32[2,2,16,1024]{3,2,1,0:T(8,128)S(1)}, u32[]{:S(2)}, u32[]{:S(2)}) collective-permute-start(f32[2,2,16,1024]{3,2,1,0:T(8,128)S(1)} %get-tuple-element.795), channel_id=1, source_target_pairs={{2,0},{4,2},{6,4},{8,6},{10,8},{12,10},{14,12},{16,14},{18,16},{20... | collective-permute-start | bytes 786440 | tf_op jit(solution)/shard_map/while/body/eval_jaxpr/ppermute | solution.py:28
  96.5 7.7 %collective-permute-start.3 = (f32[2,2,16,1024]{3,2,1,0:T(8,128)S(1)}, f32[2,2,16,1024]{3,2,1,0:T(8,128)S(1)}, u32[]{:S(2)}, u32[]{:S(2)}) collective-permute-start(f32[2,2,16,1024]{3,2,1,0:T(8,128)S(1)} %get-tuple-element.796), channel_id=1, source_target_pairs={{0,2},{2,4},{4,6},{6,8},{8,10},{10,12},{12,14},{14,16},{16,18},{18... | collective-permute-start | bytes 786440 | tf_op jit(solution)/shard_map/while/body/eval_jaxpr/ppermute | solution.py:25
  109.1 8.9 %collective-permute-start.2 = (f32[2,2,16,1024]{3,2,1,0:T(8,128)S(1)}, f32[2,2,16,1024]{3,2,1,0:T(8,128)S(1)}, u32[]{:S(2)}, u32[]{:S(2)}) collective-permute-start(f32[2,2,16,1024]{3,2,1,0:T(8,128)S(1)} %get-tuple-element.795), channel_id=1, source_target_pairs={{2,0},{4,2},{6,4},{8,6},{10,8},{12,10},{14,12},{16,14},{18,16},{20... | collective-permute-start | bytes 786440 | tf_op jit(solution)/shard_map/while/body/eval_jaxpr/ppermute | solution.py:28
  111.4 7.7 %collective-permute-start.3 = (f32[2,2,16,1024]{3,2,1,0:T(8,128)S(1)}, f32[2,2,16,1024]{3,2,1,0:T(8,128)S(1)}, u32[]{:S(2)}, u32[]{:S(2)}) collective-permute-start(f32[2,2,16,1024]{3,2,1,0:T(8,128)S(1)} %get-tuple-element.796), channel_id=1, source_target_pairs={{0,2},{2,4},{4,6},{6,8},{8,10},{10,12},{12,14},{14,16},{16,18},{18... | collective-permute-start | bytes 786440 | tf_op jit(solution)/shard_map/while/body/eval_jaxpr/ppermute | solution.py:25
  124.0 8.9 %collective-permute-start.2 = (f32[2,2,16,1024]{3,2,1,0:T(8,128)S(1)}, f32[2,2,16,1024]{3,2,1,0:T(8,128)S(1)}, u32[]{:S(2)}, u32[]{:S(2)}) collective-permute-start(f32[2,2,16,1024]{3,2,1,0:T(8,128)S(1)} %get-tuple-element.795), channel_id=1, source_target_pairs={{2,0},{4,2},{6,4},{8,6},{10,8},{12,10},{14,12},{16,14},{18,16},{20... | collective-permute-start | bytes 786440 | tf_op jit(solution)/shard_map/while/body/eval_jaxpr/ppermute | solution.py:28
  126.3 7.7 %collective-permute-start.3 = (f32[2,2,16,1024]{3,2,1,0:T(8,128)S(1)}, f32[2,2,16,1024]{3,2,1,0:T(8,128)S(1)}, u32[]{:S(2)}, u32[]{:S(2)}) collective-permute-start(f32[2,2,16,1024]{3,2,1,0:T(8,128)S(1)} %get-tuple-element.796), channel_id=1, source_target_pairs={{0,2},{2,4},{4,6},{6,8},{8,10},{10,12},{12,14},{14,16},{16,18},{18... | collective-permute-start | bytes 786440 | tf_op jit(solution)/shard_map/while/body/eval_jaxpr/ppermute | solution.py:25
  160.2 28.4 %all-to-all-start = ((f32[8,32,1024]{2,1,0:T(8,128)}), f32[8,32,1024]{2,1,0:T(8,128)S(1)}, u32[]{:S(2)}, u32[]{:S(2)}) async-start(f32[8,32,1024]{2,1,0:T(8,128)} %broadcast_in_dim.16), calls=%async_computation | async-start | bytes 2097152 | tf_op jit(solution)/shard_map/all_to_all | solution.py:35
  167.2 10.9 %collective-permute-start.18 = (f32[1,1,128]{2,1,0:T(1,128)S(1)}, f32[1,1,128]{2,1,0:T(1,128)S(1)}, u32[]{:S(2)}, u32[]{:S(2)}) collective-permute-start(f32[1,1,128]{2,1,0:T(1,128)S(1)} %get-tuple-element.603), channel_id=1, source_target_pairs={{0,2},{2,4},{4,6},{6,8},{8,10},{10,12},{12,14},{14,16},{16,18},{18... | collective-permute-start | bytes 1544 | tf_op jit(solution)/shard_map/ppermute | solution.py:25
  179.7 7.4 %collective-permute-start.21 = (f32[1,34,1]{2,1,0:T(8,128)S(1)}, f32[1,34,1]{2,1,0:T(8,128)S(1)}, u32[]{:S(2)}, u32[]{:S(2)}) collective-permute-start(f32[1,34,1]{2,1,0:T(8,128)S(1)} %get-tuple-element.597), channel_id=1, source_target_pairs={{1,0},{64,1},{65,64},{128,65},{129,128},{192,129},{193,192},{3,2},... | collective-permute-start | bytes 416 | tf_op jit(solution)/shard_map/ppermute | solution.py:28
  181.0 7.5 %collective-permute-start.20 = (f32[1,34,1]{2,1,0:T(8,128)S(1)}, f32[1,34,1]{2,1,0:T(8,128)S(1)}, u32[]{:S(2)}, u32[]{:S(2)}) collective-permute-start(f32[1,34,1]{2,1,0:T(8,128)S(1)} %get-tuple-element.598), channel_id=1, source_target_pairs={{0,1},{1,64},{64,65},{65,128},{128,129},{129,192},{192,193},{2,3},... | collective-permute-start | bytes 416 | tf_op jit(solution)/shard_map/ppermute | solution.py:25
  199.1 8.3 %collective-permute-start.9 = (f32[2,34,1]{2,1,0:T(8,128)S(1)}, f32[2,34,1]{2,1,0:T(8,128)S(1)}, u32[]{:S(2)}, u32[]{:S(2)}) collective-permute-start(f32[2,34,1]{2,1,0:T(8,128)S(1)} %get-tuple-element.589), channel_id=1, source_target_pairs={{1,0},{64,1},{65,64},{128,65},{129,128},{192,129},{193,192},{3,2},... | collective-permute-start | bytes 824 | tf_op jit(solution)/shard_map/ppermute | solution.py:28
  200.4 8.6 %collective-permute-start.8 = (f32[2,34,1]{2,1,0:T(8,128)S(1)}, f32[2,34,1]{2,1,0:T(8,128)S(1)}, u32[]{:S(2)}, u32[]{:S(2)}) collective-permute-start(f32[2,34,1]{2,1,0:T(8,128)S(1)} %get-tuple-element.590), channel_id=1, source_target_pairs={{0,1},{1,64},{64,65},{65,128},{128,129},{129,192},{192,193},{2,3},... | collective-permute-start | bytes 824 | tf_op jit(solution)/shard_map/ppermute | solution.py:25
  211.3 12.8 %collective-permute-start.11 = (f32[32,1,128]{2,0,1:T(8,128)}, f32[32,1,128]{2,0,1:T(8,128)S(1)}, u32[]{:S(2)}, u32[]{:S(2)}) collective-permute-start(f32[32,1,128]{2,0,1:T(8,128)} %bitcast.93), channel_id=1, source_target_pairs={{2,0},{4,2},{6,4},{8,6},{10,8},{12,10},{14,12},{16,14},{18,16},{20... | collective-permute-start | bytes 49160 | tf_op jit(solution)/shard_map/ppermute | solution.py:28
  213.2 7.3 %collective-permute-start.10 = (f32[32,1,128]{2,0,1:T(8,128)}, f32[32,1,128]{2,0,1:T(8,128)}, u32[]{:S(2)}, u32[]{:S(2)}) collective-permute-start(f32[32,1,128]{2,0,1:T(8,128)} %bitcast.92), channel_id=1, source_target_pairs={{0,2},{2,4},{4,6},{6,8},{8,10},{10,12},{12,14},{14,16},{16,18},{18... | collective-permute-start | bytes 49160 | tf_op jit(solution)/shard_map/ppermute | solution.py:25
  228.0 10.5 %collective-permute-start.13 = (f32[32,34,1]{1,0,2:T(8,128)S(1)}, f32[32,34,1]{1,0,2:T(8,128)S(1)}, u32[]{:S(2)}, u32[]{:S(2)}) collective-permute-start(f32[32,34,1]{1,0,2:T(8,128)S(1)} %get-tuple-element.543), channel_id=1, source_target_pairs={{1,0},{64,1},{65,64},{128,65},{129,128},{192,129},{193,192},{3,2},... | collective-permute-start | bytes 13064 | tf_op jit(solution)/shard_map/ppermute | solution.py:28
  229.4 9.1 %collective-permute-start.12 = (f32[32,34,1]{1,0,2:T(8,128)S(1)}, f32[32,34,1]{1,0,2:T(8,128)S(1)}, u32[]{:S(2)}, u32[]{:S(2)}) collective-permute-start(f32[32,34,1]{1,0,2:T(8,128)S(1)} %get-tuple-element.544), channel_id=1, source_target_pairs={{0,1},{1,64},{64,65},{65,128},{128,129},{129,192},{192,193},{2,3},... | collective-permute-start | bytes 13064 | tf_op jit(solution)/shard_map/ppermute | solution.py:25
  288.9 23.6 %collective-permute-start.15 = (f32[32,1,128]{2,0,1:T(8,128)}, f32[32,1,128]{2,0,1:T(8,128)S(1)}, u32[]{:S(2)}, u32[]{:S(2)}) collective-permute-start(f32[32,1,128]{2,0,1:T(8,128)} %bitcast.95), channel_id=1, source_target_pairs={{2,0},{4,2},{6,4},{8,6},{10,8},{12,10},{14,12},{16,14},{18,16},{20... | collective-permute-start | bytes 49160 | tf_op jit(solution)/shard_map/ppermute | solution.py:28
  290.8 18.1 %collective-permute-start.14 = (f32[32,1,128]{2,0,1:T(8,128)}, f32[32,1,128]{2,0,1:T(8,128)}, u32[]{:S(2)}, u32[]{:S(2)}) collective-permute-start(f32[32,1,128]{2,0,1:T(8,128)} %bitcast.94), channel_id=1, source_target_pairs={{0,2},{2,4},{4,6},{6,8},{8,10},{10,12},{12,14},{14,16},{16,18},{18... | collective-permute-start | bytes 49160 | tf_op jit(solution)/shard_map/ppermute | solution.py:25
  302.6 26.9 %collective-permute-start.23 = (f32[32,1,128]{2,0,1:T(8,128)}, f32[32,1,128]{2,0,1:T(8,128)}, u32[]{:S(2)}, u32[]{:S(2)}) collective-permute-start(f32[32,1,128]{2,0,1:T(8,128)} %bitcast.436), channel_id=1, source_target_pairs={{2,0},{4,2},{6,4},{8,6},{10,8},{12,10},{14,12},{16,14},{18,16},{20... | collective-permute-start | bytes 49160 | tf_op jit(solution)/shard_map/ppermute | solution.py:28
  304.5 21.4 %collective-permute-start.22 = (f32[32,1,128]{2,0,1:T(8,128)}, f32[32,1,128]{2,0,1:T(8,128)}, u32[]{:S(2)}, u32[]{:S(2)}) collective-permute-start(f32[32,1,128]{2,0,1:T(8,128)} %bitcast.437), channel_id=1, source_target_pairs={{0,2},{2,4},{4,6},{6,8},{8,10},{10,12},{12,14},{14,16},{16,18},{18... | collective-permute-start | bytes 49160 | tf_op jit(solution)/shard_map/ppermute | solution.py:25
  316.9 44.8 %collective-permute-start.17 = (f32[32,34,1]{1,0,2:T(8,128)}, f32[32,34,1]{1,0,2:T(8,128)}, u32[]{:S(2)}, u32[]{:S(2)}) collective-permute-start(f32[32,34,1]{1,0,2:T(8,128)} %get-tuple-element.539), channel_id=1, source_target_pairs={{1,0},{64,1},{65,64},{128,65},{129,128},{192,129},{193,192},{3,2},... | collective-permute-start | bytes 13064 | tf_op jit(solution)/shard_map/ppermute | solution.py:28
  318.3 43.3 %collective-permute-start.16 = (f32[32,34,1]{1,0,2:T(8,128)}, f32[32,34,1]{1,0,2:T(8,128)}, u32[]{:S(2)}, u32[]{:S(2)}) collective-permute-start(f32[32,34,1]{1,0,2:T(8,128)} %get-tuple-element.540), channel_id=1, source_target_pairs={{0,1},{1,64},{64,65},{65,128},{128,129},{129,192},{192,193},{2,3},... | collective-permute-start | bytes 13064 | tf_op jit(solution)/shard_map/ppermute | solution.py:25
  334.1 11.7 %collective-permute-start.25 = (f32[32,34,1]{1,0,2:T(8,128)S(1)}, f32[32,34,1]{1,0,2:T(8,128)S(1)}, u32[]{:S(2)}, u32[]{:S(2)}) collective-permute-start(f32[32,34,1]{1,0,2:T(8,128)S(1)} %get-tuple-element.535), channel_id=1, source_target_pairs={{1,0},{64,1},{65,64},{128,65},{129,128},{192,129},{193,192},{3,2},... | collective-permute-start | bytes 13064 | tf_op jit(solution)/shard_map/ppermute | solution.py:28
  335.6 10.3 %collective-permute-start.24 = (f32[32,34,1]{1,0,2:T(8,128)S(1)}, f32[32,34,1]{1,0,2:T(8,128)S(1)}, u32[]{:S(2)}, u32[]{:S(2)}) collective-permute-start(f32[32,34,1]{1,0,2:T(8,128)S(1)} %get-tuple-element.536), channel_id=1, source_target_pairs={{0,1},{1,64},{64,65},{65,128},{128,129},{129,192},{192,193},{2,3},... | collective-permute-start | bytes 13064 | tf_op jit(solution)/shard_map/ppermute | solution.py:25
  (53 other events, 732.1 us)
where the time goes:
time: 542 us; the launch traced here: 533 us
  local copies, waits for them, and re-layouts  169 us (31%)
  starting transfers between devices  122 us (23%)
  blocking collectives  93.2 us (17%)
  other arithmetic  73.7 us (14%)
  matrix products  37.8 us (7%)
  waiting for transfers between devices  33.1 us (6%)
    psum x5, blocking collectives, by_axis(): return functools.reduce(lax.psum, axes, x)  93.2 us
    slice x25, local copies, waits for them, and re-layouts, patches(): extended[:, down:down + height, across:across + breadth]  84.2 us
    ppermute x19, starting transfers between devices, extended_2(): lax.ppermute(lax.slice_in_dim(block, block.shape[dim] - width, None, axis...  78.5 us
    ppermute x19, starting transfers between devices, extended_2(): lax.ppermute(lax.slice_in_dim(block, 0, width, axis=dim), axis, backward)  36.6 us
    concatenate x23, other arithmetic, extended_2(): block = jnp.concatenate([low, block, high], axis=dim)  25.1 us
    ppermute x19, waiting for transfers between devices, extended_2(): lax.ppermute(lax.slice_in_dim(block, block.shape[dim] - width, None, axis...  22.4 us
    unnamed x126, local copies, waits for them, and re-layouts  22.3 us
    add x24, other arithmetic, block(): 2.0 * current[:, 4:-4] - earlier[:, 4:-4] + speed_part * laplace(current)  21.6 us
  transfers between devices with their start and end apart: 39, of which 16 were waited for; matrix products, arithmetic and copies ran while one was open for 14% of the time, Pallas kernels for 0%

commit v1 on v0

v1 whole, which is shorter than its diff:
```python
import numpy as np

import jax
import jax.numpy as jnp
from jax import lax
from jax.experimental import pallas as pl
from jax.experimental.pallas import tpu as pltpu
from jax.sharding import Mesh
from jax.sharding import PartitionSpec as P

BAND = ("band_0", "band_1", "band_2")
CHIPS = ("band_0", "band_1")
CORE = "band_2"
CELL = ("shot", "net")
SUMMED = ("shot", "band_2", "net")

coefficients = (-205.0 / 72.0, 8.0 / 5.0, -1.0 / 5.0, 8.0 / 315.0, -1.0 / 560.0)
speed_factor = 0.11
source_depth = 2
receiver_depth = 3
highest = lax.Precision.HIGHEST

STEPS = 16
CHIP = 64
WIDE = 3 * CHIP
LINE = 136
FLAT = 42 * 128
PART = 768
SIDE = 256
CH = 32
vmem_limit = 56 * 1024 * 1024
TAPS = [(down - 1) * LINE + (across - 1) for down in range(3) for across in range(3)]


def stencil_constants():
    lane = lax.broadcasted_iota(jnp.int32, (8, 128), 1)
    column = lax.broadcasted_iota(jnp.int32, (8, 128), 0) * 128 + lane
    c0, c1, c2, c3, c4 = coefficients

    def where(mask, value):
        return jnp.where(mask, jnp.float32(value), jnp.float32(0.0))

    return dict(
        low1=lane < 1,
        low3=lane < 3,
        high1=lane >= 127,
        high3=lane >= 125,
        c1u=where(column != 0, c1),
        c1v=where(column != 1023, c1),
        c2p=where((column != 1021) & (column != 1022), c2),
        c3p=where(column <= 1020, c3),
        c4p=where((column <= 1020) & (column != 0), c4),
        c2m=where((column != 1) & (column != 2), c2),
        c3m=where(column >= 3, c3),
        c4m=where((column >= 3) & (column != 1023), c4),
    )


def from_left(x, count, mask):
    turned = pltpu.roll(x, count, 1)
    return jnp.where(mask, pltpu.roll(turned, 1, 0), turned)


def from_right(x, count, mask):
    turned = pltpu.roll(x, 128 - count, 1)
    return jnp.where(mask, pltpu.roll(turned, 7, 0), turned)


def next_row(k, rows, at, prior, speed):
    x = rows[at]
    left = from_left(x, 1, k["low1"])
    right = from_right(x, 1, k["high1"])
    ahead = k["c2p"] * right + k["c3p"] * x + k["c4p"] * left
    behind = k["c2m"] * left + k["c3m"] * x + k["c4m"] * right
    total = k["c1u"] * left + k["c1v"] * right
    total = total + from_left(ahead, 3, k["low3"])
    total = total + from_right(behind, 3, k["high3"])
    vertical = (2.0 * coefficients[0]) * x
    for reach in range(1, 5):
        vertical = vertical + coefficients[reach] * (rows[at - reach] + rows[at + reach])
    return (x + x) - prior + speed * (total + vertical)


def advance(k, fields, speeds, now, step, after_core):
    other = 1 - now

    def block(first, count, store_more=None):
        rows = [fields[now, first - 4 + i] for i in range(count + 8)]
        for i in range(count):
            fresh = next_row(k, rows, i + 4, fields[other, first + i], speeds[first + i])
            fields[other, first + i] = fresh
            if store_more is not None:
                store_more(first - CHIP + i, fresh)

    reach = 4 * step

    def sides(i, carry):
        block(reach + 4 * i, 4)
        block(2 * CHIP + 4 * i, 4)
        return carry

    if step < STEPS:
        lax.fori_loop(0, STEPS - step, sides, 0)

    def core(i, carry):
        block(CHIP + 8 * i, 8, after_core)
        return carry

    lax.fori_loop(0, CHIP // 8, core, 0)


def fill(fields, speeds, low, mid, high, velocity_low, velocity_mid, velocity_high):
    for place, source, speed in (
        (0, low, velocity_low),
        (CHIP, mid, velocity_mid),
        (2 * CHIP, high, velocity_high),
    ):

        def copy(i, carry, place=place, source=source, speed=speed):
            for part in range(2):
                fields[part, pl.ds(place + 8 * i, 8)] = source[pl.ds(CHIP * part + 8 * i, 8)]
            speeds[pl.ds(place + 8 * i, 8)] = speed(8 * i)
            return carry

        lax.fori_loop(0, CHIP // 8, copy, 0)


def squared(values):
    scaled = values * speed_factor
    return scaled * scaled


def forward_kernel(pulses, source, low, mid, velocity, high, stored, speeds, fields):
    def halo_speed(ref):
        return lambda first: squared(ref[pl.ds(2 * CHIP + first, 8)])

    fill(
        fields,
        speeds,
        low,
        mid,
        high,
        halo_speed(low),
        lambda first: squared(velocity[pl.ds(first, 8)]),
        halo_speed(high),
    )
    k = stencil_constants()
    for n in range(STEPS):
        now = n % 2

        def keep(row, fresh, n=n):
            stored[n, row] = fresh

        advance(k, fields, speeds, now, n + 1, keep)
        row = CHIP + source_depth
        fresh = fields[1 - now, row] + pulses[n] * source[...]
        fields[1 - now, row] = fresh
        stored[n, source_depth] = fresh


def adjoint_kernel(counts, recorded, low, mid, high, speeds_in, stored, extra, out, fields, image, turned):
    for place, source in ((0, low), (CHIP, mid), (2 * CHIP, high)):

        def copy(i, carry, place=place, source=source):
            for part in range(2):
                fields[part, pl.ds(place + 8 * i, 8)] = source[pl.ds(CHIP * part + 8 * i, 8)]
            return carry

        lax.fori_loop(0, CHIP // 8, copy, 0)
    k = stencil_constants()

    def image_at(row):
        return (pl.ds(pl.multiple_of(row * 8, 8), 8), slice(None))

    for m in range(STEPS):
        now = m % 2
        n = STEPS - 1 - m

        def add(row, fresh, n=n, m=m):
            product = stored[n, row] * fresh
            if m:
                product = image[image_at(row)] + product
            image[image_at(row)] = product

        advance(k, fields, speeds_in, now, m + 1, add)
        row = CHIP + receiver_depth
        sample = stored[n, receiver_depth]
        push = counts[...] * sample - recorded[n]
        fields[1 - now, row] = fields[1 - now, row] + push
        place = image_at(receiver_depth)
        image[place] = image[place] + sample * push
    blank = jnp.zeros((64, 128), jnp.float32)
    for j in range(8):
        block = jnp.concatenate(
            [image[pl.ds(64 * b + j, 8, stride=8), :] for b in range(8)], axis=0
        )
        for core in range(2):
            d = ((j // 2) * 2 + core) * 2 + j % 2
            out[d, 0:40, :] = block[24 * core : 24 * core + 40]
        turned[j] = jnp.transpose(jnp.concatenate([block, blank], axis=0))
    sub = lax.broadcasted_iota(jnp.int32, (8, 128), 0)
    for j in range(8):
        edges = jnp.zeros((8, 128), jnp.float32)
        if j > 0:
            edges = jnp.where(sub < 3, pltpu.roll(turned[j - 1, 120:128, :], 3, 0), edges)
        if j < 7:
            edges = jnp.where(
                (sub >= 3) & (sub < 6), pltpu.roll(turned[j + 1, 0:8, :], 3, 0), edges
            )
        for core in range(2):
            d = ((j // 2) * 2 + core) * 2 + j % 2
            out[d, 40:48, :] = edges + extra[d]


def split(x):
    high = x.astype(jnp.bfloat16)
    low = (x - high.astype(jnp.float32)).astype(jnp.bfloat16)
    return high, low


def window(ref, rows, first, count, shift):
    start = SIDE + first + shift
    base = start // 128 * 128
    offset = start - base
    if offset == 0:
        return ref[rows, base : base + count]
    wide = ref[rows, base : base + count + 128]
    return pltpu.roll(wide, count + 128 - offset, 1)[:, :count]


def mul(left, right):
    return jnp.dot(left, right, preferred_element_type=jnp.float32)


def mul_t(left, right):
    return lax.dot_general(
        left, right, (((1,), (1,)), ((), ())), preferred_element_type=jnp.float32
    )


def network_kernel(
    core, summed, arrived, velocity_wide, cotangent_rows, inside, own, first_w, middle_w, back_w, last_w,
    new_velocity, grads,
    base, taps, packed, slope_one_d, before, products, last_products, pairs, hidden_one, slope_own, packed_two, packed_slope, own_terms, updates,
):
    lane = lax.broadcasted_iota(jnp.int32, (8, 128), 1)
    sub = lax.broadcasted_iota(jnp.int32, (8, 128), 0)
    lower = core[0] == 0
    edges = summed[40:48, :]
    other_edges = arrived[8:16, :]
    edge_rows = jnp.where(
        lower,
        jnp.where(lane < 3, pltpu.roll(other_edges, 67, 1), pltpu.roll(edges, 3, 1)),
        jnp.where(
            (lane >= 35) & (lane < 38), pltpu.roll(other_edges, 35, 1), pltpu.roll(edges, 99, 1)
        ),
    )
    turned = jnp.transpose(
        jnp.concatenate(
            [edge_rows, pltpu.roll(edges, 65, 1), jnp.zeros((112, 128), jnp.float32)], axis=0
        )
    )[0:40]
    main = summed[0:40, :]
    tile = pltpu.roll(arrived[0:8, :], 3, 0)
    down = pltpu.roll(main, 3, 0)
    up = pltpu.roll(main, 35, 0)
    low_case = jnp.concatenate([jnp.where(sub < 3, tile, down[0:8]), down[8:40]], axis=0)
    high_case = jnp.concatenate(
        [up[0:32], jnp.where((sub >= 3) & (sub < 6), tile, up[32:40])], axis=0
    )
    image = jnp.where(lower, low_case, high_case)
    lanes = lax.broadcasted_iota(jnp.int32, (40, 128), 1)
    scale = 1.0 / float(STEPS * 16) ** 0.5
    shifted = pltpu.roll(image, 3, 1)
    image_a = jnp.where(lanes < 3, turned, shifted) * scale
    image_b = jnp.where(lanes < 3, shifted, jnp.where(lanes < 6, turned, 0.0)) * scale
    shifted = pltpu.roll(cotangent_rows[...], 3, 1)
    sides = pltpu.roll(turned, 121, 1)
    cot_a = jnp.where(lanes < 1, 0.0, jnp.where(lanes < 3, sides, shifted))
    cot_b = jnp.where(lanes < 3, shifted, jnp.where(lanes < 5, sides, 0.0))
    velocity_all = velocity_wide[...]

    base[...] = jnp.zeros(base.shape, jnp.float32)
    wide_rows = [
        velocity_all,
        jnp.concatenate([image_a, image_b], axis=1),
        jnp.concatenate([cot_a, cot_b], axis=1),
    ]
    for channel, wide in enumerate(wide_rows):
        pieces = {}
        for r in range(38):
            start = LINE * r
            v, offset = start // 128, start % 128
            row = wide[r : r + 1, :]
            if offset:
                row = pltpu.roll(row, offset, 1)
            pieces.setdefault(v, []).append(row[:, 0:128])
            pieces.setdefault(v + 1, []).append(row[:, 128:256])
        for v, found in pieces.items():
            total = found[0]
            for piece in found[1:]:
                total = total + piece
            base[channel : channel + 1, SIDE + 128 * v : SIDE + 128 * v + 128] = total

    parts = [(p * PART, slice(p * PART, (p + 1) * PART)) for p in range(FLAT // PART)]
    all_rows = slice(0, 8)
    padding = jnp.zeros((8, PART), jnp.float32)
    for first, cut in parts:
        gathered = [window(base, all_rows, first, PART, shift) for shift in TAPS]
        high, low = split(jnp.concatenate(gathered + [padding], axis=0))
        taps[0:80, cut] = high
        taps[80:160, cut] = low
        result = mul(first_w[...], taps[:, cut])
        result = result[0:64] + result[64:128]
        value = result[0:CH]
        pulled = jax.nn.sigmoid(value)
        slope_one_d[:, cut] = pulled * (1.0 + value * (1.0 - pulled))
        mask = inside[:, cut] > 0.0
        mask = jnp.concatenate([mask] * 4, axis=0)
        hidden = jnp.where(mask, value * pulled, 0.0)
        hidden_one[:, SIDE + first : SIDE + first + PART] = hidden
        before[:, cut] = result[CH : 2 * CH]
        high, low = split(hidden)
        packed[0:32, cut] = high
        packed[32:64, cut] = low
        packed[64:96, cut] = high
    edge = jnp.zeros((CH, SIDE), jnp.float32)
    hidden_one[:, 0:SIDE] = edge
    hidden_one[:, SIDE + FLAT :] = edge
    zero_edge = jnp.zeros((9 * CH, SIDE), jnp.float32)
    products[:, 0:SIDE] = zero_edge
    products[:, SIDE + FLAT :] = zero_edge
    last_products[:, 0:SIDE] = jnp.zeros((16, SIDE), jnp.float32)
    last_products[:, SIDE + FLAT :] = jnp.zeros((16, SIDE), jnp.float32)

    for first, cut in parts:
        products[:, SIDE + first : SIDE + first + PART] = mul(middle_w[...], packed[:, cut])
    for first, cut in parts:
        mask = inside[:, cut] > 0.0
        here = own[:, cut] > 0.0
        for g in range(4):
            total = None
            for tap, shift in enumerate(TAPS):
                piece = window(
                    products, slice(tap * CH + 8 * g, tap * CH + 8 * g + 8), first, PART, shift
                )
                total = piece if total is None else total + piece
            pulled = jax.nn.sigmoid(total)
            rows = slice(8 * g, 8 * g + 8)
            hidden = jnp.where(mask, total * pulled, 0.0)
            slope = jnp.where(
                mask, before[rows, cut] * (pulled * (1.0 + total * (1.0 - pulled))), 0.0
            )
            pairs[rows, cut] = hidden
            slope_own[rows, cut] = slope
        hidden = pairs[:, cut]
        slope = slope_own[:, cut]
        high, low = split(hidden)
        packed_two[0:32, cut] = high
        packed_two[32:64, cut] = low
        packed_two[64:96, cut] = high
        here = jnp.concatenate([here] * 4, axis=0)
        high, low = split(jnp.where(here, hidden, 0.0))
        own_terms[32:64, cut] = high
        own_terms[96:128, cut] = low
        high, low = split(slope)
        packed_slope[0:32, cut] = high
        packed_slope[32:64, cut] = low
        packed_slope[64:96, cut] = high
        last_products[:, SIDE + first : SIDE + first + PART] = mul(last_w[...], packed_two[:, cut])

    wide_sub = lax.broadcasted_iota(jnp.int32, (8, PART), 0)
    for first, cut in parts:
        total = jnp.zeros((8, PART), jnp.float32)
        for tap, shift in enumerate(TAPS):
            rows = slice(0, 8) if tap < 8 else slice(8, 16)
            piece = window(last_products, rows, first, PART, shift)
            total = total + jnp.where(wide_sub == tap % 8, piece, 0.0)
        updates[0:1, cut] = jnp.sum(total, axis=0, keepdims=True)
    velocity_here = pltpu.roll(velocity_all, 253, 1)[:, 0:128]
    for r in range(32):
        start = LINE * (r + 3) + 3
        v, offset = start // 128, start % 128
        row = updates[0:1, 128 * v : 128 * v + 256]
        if offset:
            row = pltpu.roll(row, 256 - offset, 1)
        new_velocity[r : r + 1, :] = velocity_here[r + 3 : r + 4] + row[:, 0:128]

    for first, cut in parts:
        products[:, SIDE + first : SIDE + first + PART] = mul(back_w[...], packed_slope[:, cut])
    for first, cut in parts:
        here = own[:, cut] > 0.0
        for g in range(4):
            total = None
            for tap, shift in enumerate(TAPS):
                piece = window(
                    products, slice(tap * CH + 8 * g, tap * CH + 8 * g + 8), first, PART, -shift
                )
                total = piece if total is None else total + piece
            rows = slice(8 * g, 8 * g + 8)
            pairs[rows, cut] = jnp.where(here, total * slope_one_d[rows, cut], 0.0)
        high, low = split(pairs[:, cut])
        own_terms[0:32, cut] = high
        own_terms[64:96, cut] = low

    middle_sum = jnp.zeros((CH, 9 * CH), jnp.float32)
    outer_sum = jnp.zeros((64, 80), jnp.float32)
    for first, cut in parts:
        here = jnp.concatenate([own[:, cut] > 0.0] * 4, axis=0)
        shifted = jnp.concatenate(
            [window(hidden_one, slice(0, CH), first, PART, shift) for shift in TAPS], axis=0
        )
        high, low = split(shifted)
        slope_high, slope_low = split(jnp.where(here, slope_own[:, cut], 0.0))
        both = mul_t(jnp.concatenate([slope_high, slope_low], axis=0), high)
        middle_sum = middle_sum + (both[0:CH] + both[CH:] + mul_t(slope_high, low))
        terms = own_terms[:, cut]
        both = mul_t(terms, taps[0:80, cut])
        outer_sum = outer_sum + (both[0:64] + both[64:128] + mul_t(terms[0:64], taps[80:160, cut]))
    grads[:, 0:288] = middle_sum
    column = lax.broadcasted_iota(jnp.int32, (CH, 80), 1)
    mixed = jnp.where(column % 8 < 2, outer_sum[0:CH], outer_sum[CH:64])
    grads[:, 384:464] = mixed


def vmem():
    return pl.BlockSpec(memory_space=pltpu.VMEM)


def smem():
    return pl.BlockSpec(memory_space=pltpu.SMEM)


def f32(*shape):
    return jax.ShapeDtypeStruct(shape, jnp.float32)


def scratch(*shape, dtype=jnp.float32):
    return pltpu.VMEM(shape, dtype)


def call(kernel, in_specs, out_shape, scratch_shapes, *operands):
    many = isinstance(out_shape, tuple)
    return pl.pallas_call(
        kernel,
        in_specs=in_specs,
        out_specs=tuple(vmem() for _ in out_shape) if many else vmem(),
        out_shape=out_shape,
        scratch_shapes=scratch_shapes,
        compiler_params=pltpu.CompilerParams(vmem_limit_bytes=vmem_limit),
    )(*operands)


def stacked_weights(weights):
    high = weights.astype(jnp.bfloat16)
    low = (weights - lax.reduce_precision(weights, 8, 7)).astype(jnp.bfloat16)
    return high, low


def three_terms(weights):
    high, low = stacked_weights(weights)
    return jnp.concatenate([high, high, low], axis=1)


def over_pairs(x, axis, groups):
    return x + lax.ppermute(x, axis, [(a, b) for a, b in groups] + [(b, a) for a, b in groups])


def over_fours(x, axis, groups):
    near, far, cross = (
        lax.ppermute(x, axis, [(group[i], group[i ^ turn]) for group in groups for i in range(4)])
        for turn in (1, 2, 3)
    )
    return (x + near) + (far + cross)


def on_device(
    velocity,
    wave_now,
    wave_before,
    adjoint_last,
    adjoint_after,
    wavelet,
    source_col,
    rec_first,
    rec_last,
    rec_count,
    observed,
    conv_in,
    conv_mid,
    conv_out,
    cotangent,
):
    core = lax.axis_index(CORE)
    chip = lax.axis_index(CHIPS)
    cell = lax.axis_index(CELL)
    chips = lax.axis_size(CHIPS)
    rows_here = velocity.shape[0]
    fields = jnp.stack([wave_now, wave_before, adjoint_last, adjoint_after]).reshape(
        4, 2, rows_here, 8, 128
    )
    kept = lax.dynamic_index_in_dim(fields, core, 1, keepdims=False)
    given = lax.dynamic_index_in_dim(fields, 1 - core, 1, keepdims=False)
    shared = jnp.concatenate(
        [velocity.reshape(rows_here, 8, 128), cotangent.reshape(rows_here // 8, 8, 128)]
    )
    mine = jnp.concatenate([kept.reshape(-1, 8, 128), shared])
    theirs = lax.ppermute(
        jnp.concatenate([given.reshape(-1, 8, 128), shared]), CORE, [(0, 1), (1, 0)]
    )
    lower = core == 0
    top = jnp.where(lower, mine, theirs)
    bottom = jnp.where(lower, theirs, mine)

    def joined(first, count):
        return [top[first : first + count], bottom[first : first + count]]

    r = rows_here
    waves = jnp.concatenate(joined(0, r) + joined(r, r))
    adjoints = jnp.concatenate(joined(2 * r, r) + joined(3 * r, r))
    velocity_chip = jnp.concatenate(joined(4 * r, r))
    cot_chip = jnp.concatenate(joined(5 * r, r // 8))
    up = [(i, i + 1) for i in range(chips - 1)]
    down = [(i + 1, i) for i in range(chips - 1)]
    low = lax.ppermute(jnp.concatenate([waves, velocity_chip, cot_chip[-1:]]), CHIPS, up)
    high = lax.ppermute(jnp.concatenate([waves, velocity_chip, cot_chip[:1]]), CHIPS, down)
    low_adjoint = lax.ppermute(adjoints, CHIPS, up)
    high_adjoint = lax.ppermute(adjoints, CHIPS, down)

    def of_shot(x):
        return lax.dynamic_index_in_dim(x, core, 0, keepdims=False)

    first_chip = (chip == 0).astype(jnp.float32)
    columns = jnp.arange(1024, dtype=jnp.int32)
    source = ((columns == of_shot(source_col)).astype(jnp.float32) * first_chip).reshape(8, 128)
    slots = jnp.arange(observed.shape[2], dtype=jnp.int32)
    begin, end, count = of_shot(rec_first), of_shot(rec_last), of_shot(rec_count)
    placed = begin + slots * (end - begin) // (count - 1)
    table = ((columns[:, None] == placed[None, :]) & (slots < count)[None, :]).astype(
        jnp.float32
    ) * first_chip
    counts = jnp.sum(table, axis=1).reshape(8, 128)
    recorded = jnp.einsum("tk,wk->tw", of_shot(observed), table, precision=highest).reshape(
        -1, 8, 128
    )

    stored, speeds = call(
        forward_kernel,
        [smem()] + [vmem()] * 5,
        (f32(STEPS, CHIP, 8, 128), f32(WIDE, 8, 128)),
        [scratch(2, WIDE, 8, 128)],
        of_shot(wavelet),
        source,
        low,
        waves,
        velocity_chip,
        high,
    )

    cot_around = jnp.concatenate(
        [low[-1], cot_chip.reshape(CHIP, 128), high[-1]], axis=0
    )
    cot_rows = jnp.pad(lax.dynamic_slice_in_dim(cot_around, 32 * core + 5, 38, 0), ((0, 2), (0, 0)))
    right_edge = cot_rows[1:37, 126:128].T
    left_edge = cot_rows[1:37, 0:2].T
    to_right = jnp.pad(right_edge, ((0, 6), (64, 28)))
    to_left = jnp.pad(left_edge, ((2, 4), (64, 28)))
    targets = jnp.arange(16, dtype=jnp.int32)
    target_cell = targets // 4 * 2 + targets % 2
    same_core = targets // 2 % 2 == core
    extra = (
        jnp.where((same_core & (target_cell == cell + 1))[:, None, None], to_right[None], 0.0)
        + jnp.where((same_core & (target_cell == cell - 1))[:, None, None], to_left[None], 0.0)
    )

    velocity_all = jnp.concatenate(
        [low[2 * CHIP + CHIP - 8 : 3 * CHIP], velocity_chip, high[2 * CHIP : 2 * CHIP + 8]], axis=0
    )
    velocity_rows = lax.dynamic_slice_in_dim(velocity_all, 32 * core + 5, 38, 0).reshape(38, 1024)
    velocity_wide = lax.dynamic_slice_in_dim(
        jnp.pad(velocity_rows, ((0, 2), (3, 253))), 128 * cell, 256, 1
    )
    velocity_wide = jnp.where(jnp.arange(256)[None, :] < 134, velocity_wide, 0.0)

    place = np.arange(FLAT)
    row_of, col_of = place // LINE, place % LINE
    own = (row_of >= 3) & (row_of < 35) & (col_of >= 3) & (col_of < 131)
    own = jnp.asarray(np.broadcast_to(own.astype(np.float32), (8, FLAT)))
    in_piece = (row_of < 38) & (col_of < 134)
    grid_row = jnp.asarray(row_of, jnp.int32) + (64 * chip + 32 * core - 3)
    grid_col = jnp.asarray(col_of, jnp.int32) + (128 * cell - 3)
    inside = (
        jnp.asarray(in_piece)
        & (grid_row >= 0)
        & (grid_row < 1024)
        & (grid_col >= 0)
        & (grid_col < 1024)
    )
    inside = jnp.broadcast_to(inside.astype(jnp.float32), (8, FLAT))

    first = jnp.pad(conv_in.reshape(CH, 9, 2), ((0, 0), (0, 1), (0, 6))).reshape(CH, 80)
    pulling = jnp.pad(
        conv_out.reshape(9, CH)[::-1].T[:, :, None], ((0, 0), (0, 1), (2, 5))
    ).reshape(CH, 80)
    first_high, first_low = stacked_weights(jnp.concatenate([first, pulling]))
    first_w = jnp.concatenate(
        [
            jnp.concatenate([first_high, first_high], axis=1),
            jnp.concatenate([first_low, jnp.zeros_like(first_low)], axis=1),
        ]
    )
    middle = conv_mid.reshape(CH, 9, CH)
    middle_w = three_terms(middle.transpose(1, 0, 2).reshape(9 * CH, CH))
    back_w = three_terms(middle.transpose(1, 2, 0).reshape(9 * CH, CH))
    last_w = three_terms(jnp.pad(conv_out.reshape(9, CH), ((0, 7), (0, 0))))

    pieces = call(
        adjoint_kernel,
        [vmem()] * 8,
        f32(16, 48, 128),
        [scratch(2, WIDE, 8, 128), scratch(CHIP * 8, 128), scratch(8, 128, 128)],
        counts,
        recorded,
        low_adjoint,
        adjoints,
        high_adjoint,
        speeds,
        stored,
        extra,
    )
    summed = jnp.sum(lax.all_to_all(pieces, SUMMED, 0, 0, tiled=True), axis=0)
    edge_rows = jnp.concatenate([jnp.where(lower, summed[0:8], summed[32:40]), summed[40:48]])
    bands = lax.axis_size(BAND)
    outward = [(b, b - 1) for b in range(2, bands, 2)] + [(b, b + 1) for b in range(1, bands - 1, 2)]
    arrived = lax.ppermute(edge_rows, BAND, outward)

    bf16 = jnp.bfloat16
    new_velocity, grads = call(
        network_kernel,
        [smem()] + [vmem()] * 10,
        (f32(32, 128), f32(CH, 512)),
        [
            scratch(8, FLAT + 2 * SIDE),
            scratch(160, FLAT, dtype=bf16),
            scratch(96, FLAT, dtype=bf16),
            scratch(CH, FLAT),
            scratch(CH, FLAT),
            scratch(9 * CH, FLAT + 2 * SIDE),
            scratch(16, FLAT + 2 * SIDE),
            scratch(CH, FLAT),
            scratch(CH, FLAT + 2 * SIDE),
            scratch(CH, FLAT),
            scratch(96, FLAT, dtype=bf16),
            scratch(96, FLAT, dtype=bf16),
            scratch(128, FLAT, dtype=bf16),
            scratch(8, FLAT),
        ],
        core.reshape(1).astype(jnp.int32),
        summed,
        arrived,
        velocity_wide,
        cot_rows,
        inside,
        own,
        first_w,
        middle_w,
        back_w,
        last_w,
    )
    total = over_pairs(grads, CORE, [(0, 1)])
    total = over_fours(total, "shot", [(0, 1, 2, 3)])
    total = over_fours(total, ("band_0", "net"), [(0, 1, 2, 3)])
    total = over_fours(total, "band_1", [(0, 2, 4, 6), (1, 3, 5, 7)])
    total = over_pairs(total, "band_1", [(0, 1), (2, 3), (4, 5), (6, 7)])
    grad_mid = total[:, 0:288]
    outer = total[:, 384:456].reshape(CH, 9, 8)
    grad_in = outer[:, :, 0:2].reshape(CH, 18)
    grad_out = outer[:, ::-1, 2].T.reshape(1, 9 * CH)
    return new_velocity, grad_in, grad_mid, grad_out


def solution(mesh):
    split_mesh = Mesh(
        mesh.devices.reshape(mesh.shape["shot"], 2, 8, 2, mesh.shape["net"]),
        ("shot", "band_0", "band_1", "band_2", "net"),
    )
    placed = (
        P(BAND, None),
        P(CELL, BAND, None),
        P(CELL, BAND, None),
        P(CELL, BAND, None),
        P(CELL, BAND, None),
        P(CELL, None),
        P(CELL),
        P(CELL),
        P(CELL),
        P(CELL),
        P(CELL, None, None),
        P(),
        P(),
        P(),
        P(BAND, CELL),
    )
    return jax.shard_map(
        on_device,
        mesh=split_mesh,
        in_specs=placed,
        out_specs=(P(BAND, CELL), P(), P(), P()),
        check_vma=False,
    )
```

time: 542 us -> 215 us (0.40); the launches traced: 533 us -> 215 us
  local copies, waits for them, and re-layouts: 169 us -> 15.4 us
  Pallas kernels: 0 us -> 101 us
  blocking collectives: 93.2 us -> 0 us
  starting transfers between devices: 122 us -> 40.9 us
  other arithmetic: 73.7 us -> 10.3 us
  matrix products: 37.8 us -> 0.66 us
  waiting for transfers between devices: 33.1 us -> 43 us
    pallas_call x0 -> x3, Pallas kernels: none -> 101 us  [call(): pl.pallas_call(kernel, in_specs=in_specs, out_specs=tuple((vmem() for _ i...]
    psum x5 -> x0, blocking collectives: 93.2 us -> none  [by_axis(): return functools.reduce(lax.psum, axes, x)]
    slice x88 -> x13, local copies, waits for them, and re-layouts: 87.8 us -> 0.85 us  [the longest x1 0.62 us: on_device(): grad_mid = total[:, 0:288]]
    ppermute x38 -> x17, starting transfers between devices: 115 us -> 35.6 us  [the longest x9 21 us: over_fours(): lax.ppermute(x, axis, [(group[i], group[i ^ turn]) for group in groups fo...]
    dot_general x25 -> x1, matrix products: 37.8 us -> 0.66 us  [on_device(): jnp.einsum('tk,wk->tw', of_shot(observed), table, precision=highest)]
    add x26 -> x7, other arithmetic: 23.8 us -> 2.42 us  [the longest x2 0.86 us: over_pairs(): x + lax.ppermute(x, axis, [(a, b) for a, b in groups] + [(b, a) for a, b...]
    concatenate x23 -> x10, other arithmetic: 25.1 us -> 4.05 us  [the longest x2 1.48 us: three_terms(): return jnp.concatenate([high, high, low], axis=1)]
    ppermute x6 -> x0, local copies, waits for them, and re-layouts: 20.2 us -> none  [the longest x3 10.7 us: extended_2(): lax.ppermute(lax.slice_in_dim(block, block.shape[dim] - width, None, axis...]
  transfers between devices with their start and end apart: 39 -> 18, of which waited for: 16 -> 13; matrix products, arithmetic and copies ran while one was open for 14% -> 7% of each run, Pallas kernels for 0% -> 21%
where the time goes in v1:
time: 215 us
  Pallas kernels  101 us (47%)
  waiting for transfers between devices  43 us (20%)
  starting transfers between devices  40.9 us (19%)
  local copies, waits for them, and re-layouts  15.4 us (7%)
  other arithmetic  10.3 us (5%)
  between operations  3.27 us (2%)
    pallas_call x3, Pallas kernels, call(): pl.pallas_call(kernel, in_specs=in_specs, out_specs=tuple((vmem() for _ i...  101 us
    ppermute x9, starting transfers between devices, over_fours(): lax.ppermute(x, axis, [(group[i], group[i ^ turn]) for group in groups fo...  21 us
    ppermute x9, waiting for transfers between devices, over_fours(): lax.ppermute(x, axis, [(group[i], group[i ^ turn]) for group in groups fo...  13.3 us
    all_to_all x1, waiting for transfers between devices, on_device(): summed = jnp.sum(lax.all_to_all(pieces, SUMMED, 0, 0, tiled=True), axis=0)  10.7 us
    ppermute x1, waiting for transfers between devices, on_device(): lax.ppermute(jnp.concatenate([waves, velocity_chip, cot_chip[:1]]), CHIPS...  8.46 us
    unnamed x59, local copies, waits for them, and re-layouts  7.02 us
    all_to_all x1, starting transfers between devices, on_device(): summed = jnp.sum(lax.all_to_all(pieces, SUMMED, 0, 0, tiled=True), axis=0)  5.3 us
    ppermute x2, waiting for transfers between devices, over_pairs(): lax.ppermute(x, axis, [(a, b) for a, b in groups] + [(b, a) for a, b in g...  5.24 us
  transfers between devices with their start and end apart: 18, of which 13 were waited for; matrix products, arithmetic and copies ran while one was open for 7% of the time, Pallas kernels for 21%

profile of v1, /device:TPU:32, one launch (start us, length us, event | category | flops | bytes accessed | tf_op | source)
XLA Modules:
  0.0 214.8 jit_solution(1508017728922113592)
XLA Ops:
  0.7 1.0 copy.68
  1.7 1.0 copy.65
  2.8 1.0 copy.66
  3.8 1.0 copy.67
  4.8 0.9 copy.69
  10.5 1.3 compare_select_fusion.source
  18.6 3.8 %collective-permute-start.4 = (f32[193,8,128]{2,1,0:T(8,128)S(1)}, f32[193,8,128]{2,1,0:T(8,128)S(1)}, u32[]{:S(2)}, u32[]{:S(2)}) collective-permute-start(f32[193,8,128]{2,1,0:T(8,128)S(1)} %constant_dynamic-update-slice_fusion.7), channel_id=1, source_target_pairs={{4,0},{8,4},{12,8},{16,12},{20,16},{24,20},{28,24},{32,28},{36,32}... | collective-permute-start | bytes 2371592 | tf_op jit(solution)/shard_map/ppermute | solution.py:526
  22.4 2.1 collective-permute-start.3
  25.0 3.8 %collective-permute-start.1 = (f32[128,8,128]{2,1,0:T(8,128)S(1)}, f32[128,8,128]{2,1,0:T(8,128)S(1)}, u32[]{:S(2)}, u32[]{:S(2)}) collective-permute-start(f32[128,8,128]{2,1,0:T(8,128)S(1)} %pad_maximum_fusion.5.mid), channel_id=1, source_target_pairs={{0,4},{4,8},{8,12},{12,16},{16,20},{20,24},{24,28},{28,32},{32,36}... | collective-permute-start | bytes 1572872 | tf_op jit(solution)/shard_map/ppermute | solution.py:527
  28.9 2.0 collective-permute-start.2
  32.5 8.5 %collective-permute-done.4.high = f32[193,8,128]{2,1,0:T(8,128)S(1)} collective-permute-done((f32[193,8,128]{2,1,0:T(8,128)S(1)}, f32[193,8,128]{2,1,0:T(8,128)S(1)}, u32[]{:S(2)}, u32[]{:S(2)}) %collective-permute-start.4) | collective-permute-done | bytes 790560 | tf_op jit(solution)/shard_map/ppermute | solution.py:526
  41.0 3.7 %collective-permute-done.3.low = f32[193,8,128]{2,1,0:T(8,128)S(1)} collective-permute-done((f32[193,8,128]{2,1,0:T(8,128)S(1)}, f32[193,8,128]{2,1,0:T(8,128)S(1)}, u32[]{:S(2)}, u32[]{:S(2)}) %collective-permute-start.3) | collective-permute-done | bytes 790560 | tf_op jit(solution)/shard_map/ppermute | solution.py:525
  45.6 46.0 %shard_map.210 = (f32[16,64,8,128]{3,2,1,0:T(8,128)}, f32[192,8,128]{2,1,0:T(8,128)}) custom-call(f32[16]{0:T(128)} %fusion.36.pulses, f32[8,128]{1,0:T(8,128)} %compare_select_fusion.source, f32[193,8,128]{2,1,0:T(8,128)} %copy-done.3, f32[128,8,128]{2,1,0:T(8,128)} %pad_maximum_fusion.6.mid, f32[64,8,128]{2,1,0:T(8,128)} %pad_maximum_fusion.7.velocity, ...), custom_call_target="tpu_custom_call" | custom-call | tf_op jit(solution)/shard_map/pallas_call | solution.py:444
  93.5 46.6 %shard_map.211 = f32[16,48,128]{2,1,0:T(8,128)} custom-call(f32[8,128]{1,0:T(8,128)} %bitcast.105, f32[16,8,128]{2,1,0:T(8,128)} %copy.54.recorded, f32[128,8,128]{2,1,0:T(8,128)} %copy-done.4, f32[128,8,128]{2,1,0:T(8,128)} %copy-done.1, f32[128,8,128]{2,1,0:T(8,128)} %copy-done.5, f32[192,8,128]{2,1,0:T(8,128)} %get-tuple-element.8.speeds_in, ...), custom_call_target="tpu_custom_call" | custom-call | tf_op jit(solution)/shard_map/pallas_call | solution.py:444
  140.0 5.3 %all-to-all-start = ((f32[16,48,128]{2,1,0:T(8,128)}), f32[16,48,128]{2,1,0:T(8,128)S(1)}, u32[]{:S(2)}, u32[]{:S(2)}) async-start(f32[16,48,128]{2,1,0:T(8,128)} %shard_map.211), calls=%async_computation | async-start | bytes 786432 | tf_op jit(solution)/shard_map/all_to_all | solution.py:631
  145.7 10.7 %all-to-all-done = f32[16,48,128]{2,1,0:T(8,128)S(1)} async-done(((f32[16,48,128]{2,1,0:T(8,128)}), f32[16,48,128]{2,1,0:T(8,128)S(1)}, u32[]{:S(2)}, u32[]{:S(2)}) %all-to-all-start) | async-done | bytes 393248 | tf_op jit(solution)/shard_map/all_to_all | solution.py:631
  156.4 2.1 collective-permute-start.5
  159.9 1.5 collective-permute-done.5.arrived
  162.8 8.9 %shard_map.212 = (f32[32,128]{1,0:T(8,128)}, f32[32,512]{1,0:T(8,128)}) custom-call(s32[1]{0:T(128)} %bitcast.core, f32[48,128]{1,0:T(8,128)} %copy-done.6, f32[16,128]{1,0:T(8,128)} %copy-done.13, f32[40,256]{1,0:T(8,128)} %fusion.19.velocity_wide, f32[40,128]{1,0:T(8,128)} %pad.32.cotangent_rows, f32[8,5376]{1,0:T(8,128)} %broadcast_in_dim.65.inside, ...), custom_call_target="tpu_custom_call" | custom-call | tf_op jit(solution)/shard_map/pallas_call | solution.py:444
  172.1 1.1 collective-permute-done.6
  174.2 2.2 %collective-permute-start.8 = (f32[32,512]{1,0:T(8,128)S(1)}, f32[32,512]{1,0:T(8,128)S(1)}, u32[]{:S(2)}, u32[]{:S(2)}) collective-permute-start(f32[32,512]{1,0:T(8,128)S(1)} %add.203), channel_id=1, source_target_pairs={{0,128},{64,192},{128,0},{192,64},{1,129},{65,193},{129,1},{193,65... | collective-permute-start | bytes 196616 | tf_op jit(solution)/shard_map/ppermute | solution.py:471
  176.4 2.5 %collective-permute-start.9 = (f32[32,512]{1,0:T(8,128)S(1)}, f32[32,512]{1,0:T(8,128)S(1)}, u32[]{:S(2)}, u32[]{:S(2)}) collective-permute-start(f32[32,512]{1,0:T(8,128)S(1)} %add.203), channel_id=1, source_target_pairs={{0,192},{64,128},{128,64},{192,0},{1,193},{65,129},{129,65},{193,1... | collective-permute-start | bytes 196616 | tf_op jit(solution)/shard_map/ppermute | solution.py:471
  179.1 1.1 collective-permute-done.8
  180.2 1.7 collective-permute-done.9
  182.4 6.8 %collective-permute-start.11 = (f32[32,512]{1,0:T(8,128)S(1)}, f32[32,512]{1,0:T(8,128)S(1)}, u32[]{:S(2)}, u32[]{:S(2)}) collective-permute-start(f32[32,512]{1,0:T(8,128)S(1)} %add_add_fusion.2), channel_id=1, source_target_pairs={{0,32},{1,33},{32,0},{33,1},{2,34},{3,35},{34,2},{35,3},{4,36},{5,... | collective-permute-start | bytes 196616 | tf_op jit(solution)/shard_map/ppermute | solution.py:471
  189.2 2.3 %collective-permute-start.12 = (f32[32,512]{1,0:T(8,128)S(1)}, f32[32,512]{1,0:T(8,128)S(1)}, u32[]{:S(2)}, u32[]{:S(2)}) collective-permute-start(f32[32,512]{1,0:T(8,128)S(1)} %add_add_fusion.2), channel_id=1, source_target_pairs={{0,33},{1,32},{32,1},{33,0},{2,35},{3,34},{34,3},{35,2},{4,37},{5,... | collective-permute-start | bytes 196616 | tf_op jit(solution)/shard_map/ppermute | solution.py:471
  192.2 2.5 %collective-permute-done.12 = f32[32,512]{1,0:T(8,128)S(1)} collective-permute-done((f32[32,512]{1,0:T(8,128)S(1)}, f32[32,512]{1,0:T(8,128)S(1)}, u32[]{:S(2)}, u32[]{:S(2)}) %collective-permute-start.12) | collective-permute-done | bytes 65568 | tf_op jit(solution)/shard_map/ppermute | solution.py:471
  194.8 5.1 %collective-permute-start.14 = (f32[32,512]{1,0:T(8,128)S(1)}, f32[32,512]{1,0:T(8,128)S(1)}, u32[]{:S(2)}, u32[]{:S(2)}) collective-permute-start(f32[32,512]{1,0:T(8,128)S(1)} %add_add_fusion.1), channel_id=1, source_target_pairs={{0,16},{8,24},{16,0},{24,8},{4,20},{12,28},{20,4},{28,12},{1,17},{... | collective-permute-start | bytes 196616 | tf_op jit(solution)/shard_map/ppermute | solution.py:471
  200.0 1.3 collective-permute-start.15
  201.3 2.4 %collective-permute-done.14 = f32[32,512]{1,0:T(8,128)S(1)} collective-permute-done((f32[32,512]{1,0:T(8,128)S(1)}, f32[32,512]{1,0:T(8,128)S(1)}, u32[]{:S(2)}, u32[]{:S(2)}) %collective-permute-start.14) | collective-permute-done | bytes 65568 | tf_op jit(solution)/shard_map/ppermute | solution.py:471
  203.7 4.8 %collective-permute-done.15 = f32[32,512]{1,0:T(8,128)S(1)} collective-permute-done((f32[32,512]{1,0:T(8,128)S(1)}, f32[32,512]{1,0:T(8,128)S(1)}, u32[]{:S(2)}, u32[]{:S(2)}) %collective-permute-start.15) | collective-permute-done | bytes 65568 | tf_op jit(solution)/shard_map/ppermute | solution.py:471
  208.7 4.1 %collective-permute-done.16 = f32[32,512]{1,0:T(8,128)S(1)} collective-permute-done((f32[32,512]{1,0:T(8,128)S(1)}, f32[32,512]{1,0:T(8,128)S(1)}, u32[]{:S(2)}, u32[]{:S(2)}) %collective-permute-start.16) | collective-permute-done | bytes 65568 | tf_op jit(solution)/shard_map/ppermute | solution.py:466
  (147 shorter events, 22.3 us)
Async XLA Ops:
  0.6 13.2 %copy-start = (f32[2,16,128]{2,1,0:T(8,128)S(1)}, f32[2,16,128]{2,1,0:T(8,128)}, u32[]{:S(2)}) copy-start(f32[2,16,128]{2,1,0:T(8,128)} %param.29) | copy-start | bytes 49156
  0.7 7.3 %copy-start.8 = (f32[32,288]{1,0:T(8,128)S(1)}, f32[32,288]{1,0:T(8,128)}, u32[]{:S(2)}) copy-start(f32[32,288]{1,0:T(8,128)} %param.31) | copy-start | bytes 110596
  1.7 6.6 %copy-start.15 = (f32[1,288]{1,0:T(1,128)S(1)}, f32[1,288]{1,0:T(1,128)}, u32[]{:S(2)}) copy-start(f32[1,288]{1,0:T(1,128)} %param.32) | copy-start | bytes 3460
  1.7 6.8 %copy-start.12 = (f32[32,18]{0,1:T(8,128)S(1)}, f32[32,18]{0,1:T(8,128)}, u32[]{:S(2)}) copy-start(f32[32,18]{0,1:T(8,128)} %param.30) | copy-start | bytes 6916
  2.8 6.6 %copy-start.19 = (s32[2]{0:T(128)S(1)}, s32[2]{0:T(128)}, u32[]{:S(2)}) copy-start(s32[2]{0:T(128)} %param.26) | copy-start | bytes 28
  2.8 7.2 %copy-start.20 = (s32[2]{0:T(128)S(1)}, s32[2]{0:T(128)}, u32[]{:S(2)}) copy-start(s32[2]{0:T(128)} %param.27) | copy-start | bytes 28
  6.0 12.3 %collective-permute-start = (f32[164,8,128]{2,1,0:T(8,128)S(1)}, f32[164,8,128]{2,1,0:T(8,128)S(1)}, u32[]{:S(2)}, u32[]{:S(2)}) collective-permute-start(f32[164,8,128]{2,1,0:T(8,128)S(1)} %pad_maximum_fusion.1), channel_id=1, source_target_pairs={{0,2},{2,0},{1,3},{3,1},{4,6},{6,4},{5,7},{7,5},{8,10},{10,8},{9,1... | collective-permute-start | bytes 2015240 | tf_op jit(solution)/shard_map/ppermute | solution.py:508
  17.4 7.1 %copy-start.16 = (f32[2,16]{1,0:T(2,128)S(1)}, f32[2,16]{1,0:T(2,128)}, u32[]{:S(2)}) copy-start(f32[2,16]{1,0:T(2,128)} %param.24) | copy-start | bytes 388
  18.6 22.4 %collective-permute-start.4 = (f32[193,8,128]{2,1,0:T(8,128)S(1)}, f32[193,8,128]{2,1,0:T(8,128)S(1)}, u32[]{:S(2)}, u32[]{:S(2)}) collective-permute-start(f32[193,8,128]{2,1,0:T(8,128)S(1)} %constant_dynamic-update-slice_fusion.7), channel_id=1, source_target_pairs={{4,0},{8,4},{12,8},{16,12},{20,16},{24,20},{28,24},{32,28},{36,32}... | collective-permute-start | bytes 2371592 | tf_op jit(solution)/shard_map/ppermute | solution.py:526
  22.4 22.4 %collective-permute-start.3 = (f32[193,8,128]{2,1,0:T(8,128)S(1)}, f32[193,8,128]{2,1,0:T(8,128)S(1)}, u32[]{:S(2)}, u32[]{:S(2)}) collective-permute-start(f32[193,8,128]{2,1,0:T(8,128)S(1)} %constant_dynamic-update-slice_fusion), channel_id=1, source_target_pairs={{0,4},{4,8},{8,12},{12,16},{16,20},{20,24},{24,28},{28,32},{32,36}... | collective-permute-start | bytes 2371592 | tf_op jit(solution)/shard_map/ppermute | solution.py:525
  25.0 67.4 %copy-start.1 = (f32[128,8,128]{2,1,0:T(8,128)}, f32[128,8,128]{2,1,0:T(8,128)S(1)}, u32[]{:S(2)}) copy-start(f32[128,8,128]{2,1,0:T(8,128)S(1)} %pad_maximum_fusion.5.mid) | copy-start | bytes 1572868
  25.0 67.3 %collective-permute-start.1 = (f32[128,8,128]{2,1,0:T(8,128)S(1)}, f32[128,8,128]{2,1,0:T(8,128)S(1)}, u32[]{:S(2)}, u32[]{:S(2)}) collective-permute-start(f32[128,8,128]{2,1,0:T(8,128)S(1)} %pad_maximum_fusion.5.mid), channel_id=1, source_target_pairs={{0,4},{4,8},{8,12},{12,16},{16,20},{20,24},{24,28},{28,32},{32,36}... | collective-permute-start | bytes 1572872 | tf_op jit(solution)/shard_map/ppermute | solution.py:527
  28.9 63.5 %collective-permute-start.2 = (f32[128,8,128]{2,1,0:T(8,128)S(1)}, f32[128,8,128]{2,1,0:T(8,128)S(1)}, u32[]{:S(2)}, u32[]{:S(2)}) collective-permute-start(f32[128,8,128]{2,1,0:T(8,128)S(1)} %pad_maximum_fusion.5.mid), channel_id=1, source_target_pairs={{4,0},{8,4},{12,8},{16,12},{20,16},{24,20},{28,24},{32,28},{36,32}... | collective-permute-start | bytes 1572872 | tf_op jit(solution)/shard_map/ppermute | solution.py:528
  91.6 53.7 %copy-start.10 = (s32[5376]{0:T(1024)S(1)}, s32[5376]{0:T(1024)}, u32[]{:S(2)}) copy-start(s32[5376]{0:T(1024)} %constant.148.clone) | copy-start | bytes 64516
  91.6 53.7 %copy-start.11 = (s32[5376]{0:T(1024)S(1)}, s32[5376]{0:T(1024)}, u32[]{:S(2)}) copy-start(s32[5376]{0:T(1024)} %constant.149.clone) | copy-start | bytes 64516
  91.6 53.7 %copy-start.14 = (pred[5376]{0:T(1024)(128)(4,1)S(1)}, pred[5376]{0:T(1024)(128)(4,1)}, u32[]{:S(2)}) copy-start(pred[5376]{0:T(1024)(128)(4,1)} %constant.150.clone) | copy-start | bytes 16132
  91.7 53.8 %slice-start = ((f32[193,8,128]{2,1,0:T(8,128)}), f32[8,8,128]{2,1,0:T(8,128)S(1)}, s32[]{:S(2)}) async-start(f32[193,8,128]{2,1,0:T(8,128)} %copy-done.2), calls=%async_computation.1 | async-start | bytes 65536 | tf_op jit(solution)/shard_map/slice | solution.py:577
  91.7 53.8 %slice-start.1 = ((f32[193,8,128]{2,1,0:T(8,128)}), f32[8,8,128]{2,1,0:T(8,128)S(1)}, s32[]{:S(2)}) async-start(f32[193,8,128]{2,1,0:T(8,128)} %copy-done.3), calls=%async_computation.2 | async-start | bytes 65536 | tf_op jit(solution)/shard_map/slice | solution.py:577
  93.5 68.6 %copy-start.9 = (f32[5376]{0:T(1024)S(1)}, f32[5376]{0:T(1024)}, u32[]{:S(2)}) copy-start(f32[5376]{0:T(1024)} %constant.147.clone) | copy-start | bytes 64516
  140.0 16.3 %all-to-all-start = ((f32[16,48,128]{2,1,0:T(8,128)}), f32[16,48,128]{2,1,0:T(8,128)S(1)}, u32[]{:S(2)}, u32[]{:S(2)}) async-start(f32[16,48,128]{2,1,0:T(8,128)} %shard_map.211), calls=%async_computation | async-start | bytes 786432 | tf_op jit(solution)/shard_map/all_to_all | solution.py:631
  156.4 5.0 %collective-permute-start.5 = (f32[16,128]{1,0:T(8,128)S(1)}, f32[16,128]{1,0:T(8,128)S(1)}, u32[]{:S(2)}, u32[]{:S(2)}) collective-permute-start(f32[16,128]{1,0:T(8,128)S(1)} %pad_maximum_fusion.11), channel_id=1, source_target_pairs={{4,2},{8,6},{12,10},{16,14},{20,18},{24,22},{28,26},{32,30},{36,34... | collective-permute-start | bytes 24584 | tf_op jit(solution)/shard_map/ppermute | solution.py:635
  171.7 1.6 collective-permute-start.6
  174.1 5.0 %collective-permute-start.7 = (f32[32,512]{1,0:T(8,128)S(1)}, f32[32,512]{1,0:T(8,128)S(1)}, u32[]{:S(2)}, u32[]{:S(2)}) collective-permute-start(f32[32,512]{1,0:T(8,128)S(1)} %add.203), channel_id=1, source_target_pairs={{0,64},{64,0},{128,192},{192,128},{1,65},{65,1},{129,193},{193,129... | collective-permute-start | bytes 196616 | tf_op jit(solution)/shard_map/ppermute | solution.py:471
  174.2 6.0 %collective-permute-start.8 = (f32[32,512]{1,0:T(8,128)S(1)}, f32[32,512]{1,0:T(8,128)S(1)}, u32[]{:S(2)}, u32[]{:S(2)}) collective-permute-start(f32[32,512]{1,0:T(8,128)S(1)} %add.203), channel_id=1, source_target_pairs={{0,128},{64,192},{128,0},{192,64},{1,129},{65,193},{129,1},{193,65... | collective-permute-start | bytes 196616 | tf_op jit(solution)/shard_map/ppermute | solution.py:471
  176.4 5.5 %collective-permute-start.9 = (f32[32,512]{1,0:T(8,128)S(1)}, f32[32,512]{1,0:T(8,128)S(1)}, u32[]{:S(2)}, u32[]{:S(2)}) collective-permute-start(f32[32,512]{1,0:T(8,128)S(1)} %add.203), channel_id=1, source_target_pairs={{0,192},{64,128},{128,64},{192,0},{1,193},{65,129},{129,65},{193,1... | collective-permute-start | bytes 196616 | tf_op jit(solution)/shard_map/ppermute | solution.py:471
  181.9 9.6 %collective-permute-start.10 = (f32[32,512]{1,0:T(8,128)S(1)}, f32[32,512]{1,0:T(8,128)S(1)}, u32[]{:S(2)}, u32[]{:S(2)}) collective-permute-start(f32[32,512]{1,0:T(8,128)S(1)} %add_add_fusion.2), channel_id=1, source_target_pairs={{0,1},{1,0},{32,33},{33,32},{2,3},{3,2},{34,35},{35,34},{4,5},{5,4... | collective-permute-start | bytes 196616 | tf_op jit(solution)/shard_map/ppermute | solution.py:471
  182.4 9.8 %collective-permute-start.11 = (f32[32,512]{1,0:T(8,128)S(1)}, f32[32,512]{1,0:T(8,128)S(1)}, u32[]{:S(2)}, u32[]{:S(2)}) collective-permute-start(f32[32,512]{1,0:T(8,128)S(1)} %add_add_fusion.2), channel_id=1, source_target_pairs={{0,32},{1,33},{32,0},{33,1},{2,34},{3,35},{34,2},{35,3},{4,36},{5,... | collective-permute-start | bytes 196616 | tf_op jit(solution)/shard_map/ppermute | solution.py:471
  189.2 5.5 %collective-permute-start.12 = (f32[32,512]{1,0:T(8,128)S(1)}, f32[32,512]{1,0:T(8,128)S(1)}, u32[]{:S(2)}, u32[]{:S(2)}) collective-permute-start(f32[32,512]{1,0:T(8,128)S(1)} %add_add_fusion.2), channel_id=1, source_target_pairs={{0,33},{1,32},{32,1},{33,0},{2,35},{3,34},{34,3},{35,2},{4,37},{5,... | collective-permute-start | bytes 196616 | tf_op jit(solution)/shard_map/ppermute | solution.py:471
  194.7 6.6 %collective-permute-start.13 = (f32[32,512]{1,0:T(8,128)S(1)}, f32[32,512]{1,0:T(8,128)S(1)}, u32[]{:S(2)}, u32[]{:S(2)}) collective-permute-start(f32[32,512]{1,0:T(8,128)S(1)} %add_add_fusion.1), channel_id=1, source_target_pairs={{0,8},{8,0},{16,24},{24,16},{4,12},{12,4},{20,28},{28,20},{1,9},{9... | collective-permute-start | bytes 196616 | tf_op jit(solution)/shard_map/ppermute | solution.py:471
  194.8 8.9 %collective-permute-start.14 = (f32[32,512]{1,0:T(8,128)S(1)}, f32[32,512]{1,0:T(8,128)S(1)}, u32[]{:S(2)}, u32[]{:S(2)}) collective-permute-start(f32[32,512]{1,0:T(8,128)S(1)} %add_add_fusion.1), channel_id=1, source_target_pairs={{0,16},{8,24},{16,0},{24,8},{4,20},{12,28},{20,4},{28,12},{1,17},{... | collective-permute-start | bytes 196616 | tf_op jit(solution)/shard_map/ppermute | solution.py:471
  200.0 8.5 %collective-permute-start.15 = (f32[32,512]{1,0:T(8,128)S(1)}, f32[32,512]{1,0:T(8,128)S(1)}, u32[]{:S(2)}, u32[]{:S(2)}) collective-permute-start(f32[32,512]{1,0:T(8,128)S(1)} %add_add_fusion.1), channel_id=1, source_target_pairs={{0,24},{8,16},{16,8},{24,0},{4,28},{12,20},{20,12},{28,4},{1,25},{... | collective-permute-start | bytes 196616 | tf_op jit(solution)/shard_map/ppermute | solution.py:471
  208.5 4.4 %collective-permute-start.16 = (f32[32,512]{1,0:T(8,128)S(1)}, f32[32,512]{1,0:T(8,128)S(1)}, u32[]{:S(2)}, u32[]{:S(2)}) collective-permute-start(f32[32,512]{1,0:T(8,128)S(1)} %add_add_fusion), channel_id=1, source_target_pairs={{0,4},{8,12},{16,20},{24,28},{4,0},{12,8},{20,16},{28,24},{1,5},{9... | collective-permute-start | bytes 196616 | tf_op jit(solution)/shard_map/ppermute | solution.py:466
  (9 other events, 31.3 us)

commit v2 on v1

--- a/solution.py
+++ b/solution.py
@@ -22,6 +22,8 @@
 
 STEPS = 16
 CHIP = 64
+BLOCK = 32
+WAVES = 98
 WIDE = 3 * CHIP
 LINE = 136
 FLAT = 42 * 128
@@ -66,137 +68,128 @@
     return jnp.where(mask, pltpu.roll(turned, 7, 0), turned)
 
 
-def next_row(k, rows, at, prior, speed):
-    x = rows[at]
-    left = from_left(x, 1, k["low1"])
-    right = from_right(x, 1, k["high1"])
-    ahead = k["c2p"] * right + k["c3p"] * x + k["c4p"] * left
-    behind = k["c2m"] * left + k["c3m"] * x + k["c4m"] * right
-    total = k["c1u"] * left + k["c1v"] * right
-    total = total + from_left(ahead, 3, k["low3"])
-    total = total + from_right(behind, 3, k["high3"])
-    vertical = (2.0 * coefficients[0]) * x
-    for reach in range(1, 5):
-        vertical = vertical + coefficients[reach] * (rows[at - reach] + rows[at + reach])
-    return (x + x) - prior + speed * (total + vertical)
-
-
-def advance(k, fields, speeds, now, step, after_core):
+def advance(k, fields, speeds, now, step):
     other = 1 - now
-
-    def block(first, count, store_more=None):
+    c0, c1, c2, c3, c4 = coefficients
+
+    def block(first, count):
         rows = [fields[now, first - 4 + i] for i in range(count + 8)]
+        prior = [fields[other, first + i] for i in range(count)]
+        speed = [speeds[first + i] for i in range(count)]
+        middle = rows[4 : 4 + count]
+        left = [from_left(x, 1, k["low1"]) for x in middle]
+        right = [from_right(x, 1, k["high1"]) for x in middle]
+        ahead = [
+            k["c2p"] * right[i] + k["c3p"] * middle[i] + k["c4p"] * left[i] for i in range(count)
+        ]
+        behind = [
+            k["c2m"] * left[i] + k["c3m"] * middle[i] + k["c4m"] * right[i] for i in range(count)
+        ]
+        ahead = [from_left(x, 3, k["low3"]) for x in ahead]
+        behind = [from_right(x, 3, k["high3"]) for x in behind]
+        fresh = []
         for i in range(count):
-            fresh = next_row(k, rows, i + 4, fields[other, first + i], speeds[first + i])
-            fields[other, first + i] = fresh
-            if store_more is not None:
-                store_more(first - CHIP + i, fresh)
-
-    reach = 4 * step
-
-    def sides(i, carry):
-        block(reach + 4 * i, 4)
-        block(2 * CHIP + 4 * i, 4)
+            total = k["c1u"] * left[i] + k["c1v"] * right[i] + (2.0 * c0) * middle[i]
+            for reach, weight in ((1, c1), (2, c2), (3, c3), (4, c4)):
+                total = total + weight * (rows[i + 4 - reach] + rows[i + 4 + reach])
+            total = total + (ahead[i] + behind[i])
+            fresh.append((middle[i] + middle[i]) - prior[i] + speed[i] * total)
+        for i in range(count):
+            fields[other, first + i] = fresh[i]
+
+    first, count = 4 * step, WIDE - 8 * step
+    whole = count // BLOCK
+
+    def body(i, carry):
+        block(first + BLOCK * i, BLOCK)
         return carry
 
-    if step < STEPS:
-        lax.fori_loop(0, STEPS - step, sides, 0)
-
-    def core(i, carry):
-        block(CHIP + 8 * i, 8, after_core)
-        return carry
-
-    lax.fori_loop(0, CHIP // 8, core, 0)
-
-
-def fill(fields, speeds, low, mid, high, velocity_low, velocity_mid, velocity_high):
-    for place, source, speed in (
-        (0, low, velocity_low),
-        (CHIP, mid, velocity_mid),
-        (2 * CHIP, high, velocity_high),
-    ):
-
-        def copy(i, carry, place=place, source=source, speed=speed):
-            for part in range(2):
-                fields[part, pl.ds(place + 8 * i, 8)] = source[pl.ds(CHIP * part + 8 * i, 8)]
-            speeds[pl.ds(place + 8 * i, 8)] = speed(8 * i)
+    lax.fori_loop(0, whole, body, 0)
+    if count % BLOCK:
+        block(first + BLOCK * whole, count % BLOCK)
+
+
+def place_rows(core, pack, stride, put):
+    for part in range(2):
+        band = core if part == 0 else 1 - core
+
+        def copy(i, carry, part=part, band=band):
+            put(32 * band + 8 * i, lambda at: pack[pl.ds(stride * part + at + 8 * i, 8)])
             return carry
 
-        lax.fori_loop(0, CHIP // 8, copy, 0)
-
-
-def squared(values):
-    scaled = values * speed_factor
-    return scaled * scaled
-
-
-def forward_kernel(pulses, source, low, mid, velocity, high, stored, speeds, fields):
-    def halo_speed(ref):
-        return lambda first: squared(ref[pl.ds(2 * CHIP + first, 8)])
-
-    fill(
-        fields,
-        speeds,
-        low,
-        mid,
-        high,
-        halo_speed(low),
-        lambda first: squared(velocity[pl.ds(first, 8)]),
-        halo_speed(high),
-    )
+        lax.fori_loop(0, 4, copy, 0)
+
+
+def forward_kernel(
+    core_ref, pulses, source, low, mid, high, stored, speeds, velocity_rows, fields, velocity
+):
+    core = core_ref[0]
+    for place, pack in ((0, low), (CHIP, mid), (2 * CHIP, high)):
+
+        def put(row, rows_at, place=place):
+            fields[0, pl.ds(place + row, 8)] = rows_at(0)
+            fields[1, pl.ds(place + row, 8)] = rows_at(32)
+            values = rows_at(64)
+            velocity[pl.ds(place + row, 8)] = values
+            scaled = values * speed_factor
+            speeds[pl.ds(place + row, 8)] = scaled * scaled
+
+        place_rows(core, pack, WAVES, put)
+    for i in range(5):
+        velocity_rows[8 * i : 8 * i + 8] = velocity[pl.ds(CHIP - 3 + 32 * core + 8 * i, 8)]
     k = stencil_constants()
     for n in range(STEPS):
         now = n % 2
-
-        def keep(row, fresh, n=n):
-            stored[n, row] = fresh
-
-        advance(k, fields, speeds, now, n + 1, keep)
+        advance(k, fields, speeds, now, n + 1)
         row = CHIP + source_depth
-        fresh = fields[1 - now, row] + pulses[n] * source[...]
-        fields[1 - now, row] = fresh
-        stored[n, source_depth] = fresh
-
-
-def adjoint_kernel(counts, recorded, low, mid, high, speeds_in, stored, extra, out, fields, image, turned):
-    for place, source in ((0, low), (CHIP, mid), (2 * CHIP, high)):
-
-        def copy(i, carry, place=place, source=source):
+        fields[1 - now, row] = fields[1 - now, row] + pulses[n] * source[...]
+
+        def keep(i, carry, n=n, now=now):
             for part in range(2):
-                fields[part, pl.ds(place + 8 * i, 8)] = source[pl.ds(CHIP * part + 8 * i, 8)]
+                at = 8 * (2 * i + part)
+                stored[n, pl.ds(at, 8)] = fields[1 - now, pl.ds(CHIP + at, 8)]
             return carry
 
-        lax.fori_loop(0, CHIP // 8, copy, 0)
+        lax.fori_loop(0, 4, keep, 0)
+
+
+def adjoint_kernel(core_ref, counts, recorded, low, mid, high, speeds, stored, extra, out, fields, image3, turned):
+    core = core_ref[0]
+    for place, pack in ((0, low), (CHIP, mid), (2 * CHIP, high)):
+
+        def put(row, rows_at, place=place):
+            fields[0, pl.ds(place + row, 8)] = rows_at(0)
+            fields[1, pl.ds(place + row, 8)] = rows_at(32)
+
+        place_rows(core, pack, CHIP, put)
     k = stencil_constants()
-
-    def image_at(row):
-        return (pl.ds(pl.multiple_of(row * 8, 8), 8), slice(None))
-
     for m in range(STEPS):
         now = m % 2
         n = STEPS - 1 - m
-
-        def add(row, fresh, n=n, m=m):
-            product = stored[n, row] * fresh
-            if m:
-                product = image[image_at(row)] + product
-            image[image_at(row)] = product
-
-        advance(k, fields, speeds_in, now, m + 1, add)
+        advance(k, fields, speeds, now, m + 1)
         row = CHIP + receiver_depth
-        sample = stored[n, receiver_depth]
-        push = counts[...] * sample - recorded[n]
+        push = counts[...] * stored[n, receiver_depth] - recorded[n]
         fields[1 - now, row] = fields[1 - now, row] + push
-        place = image_at(receiver_depth)
-        image[place] = image[place] + sample * push
+
+        def add(i, carry, n=n, m=m, now=now):
+            for part in range(2):
+                at = 8 * (2 * i + part)
+                product = stored[n, pl.ds(at, 8)] * fields[1 - now, pl.ds(CHIP + at, 8)]
+                if m:
+                    product = image3[pl.ds(at, 8)] + product
+                image3[pl.ds(at, 8)] = product
+            return carry
+
+        lax.fori_loop(0, 4, add, 0)
+    image = image3.reshape(CHIP * 8, 128)
     blank = jnp.zeros((64, 128), jnp.float32)
     for j in range(8):
         block = jnp.concatenate(
             [image[pl.ds(64 * b + j, 8, stride=8), :] for b in range(8)], axis=0
         )
-        for core in range(2):
-            d = ((j // 2) * 2 + core) * 2 + j % 2
-            out[d, 0:40, :] = block[24 * core : 24 * core + 40]
+        for half in range(2):
+            d = ((j // 2) * 2 + half) * 2 + j % 2
+            out[d, 0:40, :] = block[24 * half : 24 * half + 40]
         turned[j] = jnp.transpose(jnp.concatenate([block, blank], axis=0))
     sub = lax.broadcasted_iota(jnp.int32, (8, 128), 0)
     for j in range(8):
@@ -207,9 +200,22 @@
             edges = jnp.where(
                 (sub >= 3) & (sub < 6), pltpu.roll(turned[j + 1, 0:8, :], 3, 0), edges
             )
-        for core in range(2):
-            d = ((j // 2) * 2 + core) * 2 + j % 2
+        for half in range(2):
+            d = ((j // 2) * 2 + half) * 2 + j % 2
             out[d, 40:48, :] = edges + extra[d]
+
+
+def pack_kernel(core_ref, now, before, last, after, velocity, cotangent, mine, given):
+    core = core_ref[0]
+    for which, out in ((core, mine), (1 - core, given)):
+        for ref, first in ((now, 0), (before, 32), (velocity, 64), (last, WAVES), (after, WAVES + 32)):
+            for b in range(4):
+                for s in range(8):
+                    rows, lanes = slice(8 * b, 8 * b + 8), slice(128 * s, 128 * s + 128)
+                    tile = ref[rows, lanes] if ref is velocity else ref[which, rows, lanes]
+                    out[pl.ds(8 * (first + 8 * b) + s, 8, stride=8), :] = tile
+        for b, at in ((0, WAVES - 2), (3, WAVES - 1), (1, WAVES + 64), (2, WAVES + 65)):
+            out[8 * at : 8 * at + 8, :] = cotangent[8 * b : 8 * b + 8, :]
 
 
 def split(x):
@@ -417,10 +423,12 @@
         terms = own_terms[:, cut]
         both = mul_t(terms, taps[0:80, cut])
         outer_sum = outer_sum + (both[0:64] + both[64:128] + mul_t(terms[0:64], taps[80:160, cut]))
-    grads[:, 0:288] = middle_sum
     column = lax.broadcasted_iota(jnp.int32, (CH, 80), 1)
     mixed = jnp.where(column % 8 < 2, outer_sum[0:CH], outer_sum[CH:64])
-    grads[:, 384:464] = mixed
+    mixed = pltpu.roll(jnp.concatenate([mixed, jnp.zeros((CH, 48), jnp.float32)], axis=1), 32, 1)
+    grads[:, 0:256] = middle_sum[:, 0:256]
+    tail = jnp.concatenate([middle_sum[:, 256:288], jnp.zeros((CH, 96), jnp.float32)], axis=1)
+    grads[:, 256:384] = tail + mixed
 
 
 def vmem():
@@ -495,37 +503,36 @@
     chip = lax.axis_index(CHIPS)
     cell = lax.axis_index(CELL)
     chips = lax.axis_size(CHIPS)
-    rows_here = velocity.shape[0]
-    fields = jnp.stack([wave_now, wave_before, adjoint_last, adjoint_after]).reshape(
-        4, 2, rows_here, 8, 128
-    )
-    kept = lax.dynamic_index_in_dim(fields, core, 1, keepdims=False)
-    given = lax.dynamic_index_in_dim(fields, 1 - core, 1, keepdims=False)
-    shared = jnp.concatenate(
-        [velocity.reshape(rows_here, 8, 128), cotangent.reshape(rows_here // 8, 8, 128)]
-    )
-    mine = jnp.concatenate([kept.reshape(-1, 8, 128), shared])
-    theirs = lax.ppermute(
-        jnp.concatenate([given.reshape(-1, 8, 128), shared]), CORE, [(0, 1), (1, 0)]
-    )
-    lower = core == 0
-    top = jnp.where(lower, mine, theirs)
-    bottom = jnp.where(lower, theirs, mine)
-
-    def joined(first, count):
-        return [top[first : first + count], bottom[first : first + count]]
-
-    r = rows_here
-    waves = jnp.concatenate(joined(0, r) + joined(r, r))
-    adjoints = jnp.concatenate(joined(2 * r, r) + joined(3 * r, r))
-    velocity_chip = jnp.concatenate(joined(4 * r, r))
-    cot_chip = jnp.concatenate(joined(5 * r, r // 8))
+    core_id = core.reshape(1).astype(jnp.int32)
+    packed_rows = WAVES + 66
+    mine, given = call(
+        pack_kernel,
+        [smem()] + [vmem()] * 6,
+        (f32(packed_rows * 8, 128), f32(packed_rows * 8, 128)),
+        [],
+        core_id,
+        wave_now,
+        wave_before,
+        adjoint_last,
+        adjoint_after,
+        velocity,
+        cotangent,
+    )
+    mine = mine.reshape(packed_rows, 8, 128)
+    theirs = lax.ppermute(given.reshape(packed_rows, 8, 128), CORE, [(0, 1), (1, 0)])
+    waves = jnp.concatenate([mine[:WAVES], theirs[:WAVES]])
     up = [(i, i + 1) for i in range(chips - 1)]
     down = [(i + 1, i) for i in range(chips - 1)]
-    low = lax.ppermute(jnp.concatenate([waves, velocity_chip, cot_chip[-1:]]), CHIPS, up)
-    high = lax.ppermute(jnp.concatenate([waves, velocity_chip, cot_chip[:1]]), CHIPS, down)
-    low_adjoint = lax.ppermute(adjoints, CHIPS, up)
-    high_adjoint = lax.ppermute(adjoints, CHIPS, down)
+    low = lax.ppermute(waves, CHIPS, up)
+    high = lax.ppermute(waves, CHIPS, down)
+    (
+        mine, theirs, wavelet, source_col, rec_first, rec_last, rec_count, observed, conv_in, conv_mid, conv_out, core, chip, cell,
+    ) = lax.optimization_barrier(
+        (
+            mine, theirs, wavelet, source_col, rec_first, rec_last, rec_count, observed, conv_in, conv_mid, conv_out, core, chip, cell,
+        )
+    )
+    lower = core == 0
 
     def of_shot(x):
         return lax.dynamic_index_in_dim(x, core, 0, keepdims=False)
@@ -544,21 +551,40 @@
         -1, 8, 128
     )
 
-    stored, speeds = call(
+    adjoints = jnp.concatenate([mine[WAVES : WAVES + 64], theirs[WAVES : WAVES + 64]])
+    adjoints, counts, recorded, source = lax.optimization_barrier(
+        (adjoints, counts, recorded, source)
+    )
+    low_adjoint = lax.ppermute(adjoints, CHIPS, up)
+    high_adjoint = lax.ppermute(adjoints, CHIPS, down)
+
+    stored, speeds, velocity_rows = call(
         forward_kernel,
-        [smem()] + [vmem()] * 5,
-        (f32(STEPS, CHIP, 8, 128), f32(WIDE, 8, 128)),
-        [scratch(2, WIDE, 8, 128)],
+        [smem()] * 2 + [vmem()] * 4,
+        (f32(STEPS, CHIP, 8, 128), f32(WIDE, 8, 128), f32(40, 8, 128)),
+        [scratch(2, WIDE, 8, 128), scratch(WIDE, 8, 128)],
+        core_id,
         of_shot(wavelet),
         source,
         low,
         waves,
-        velocity_chip,
         high,
     )
 
+    def cot_of(pack):
+        return [pack[WAVES - 2], pack[WAVES + 64], pack[WAVES + 65], pack[WAVES - 1]]
+
+    cot_mine = jnp.concatenate(cot_of(mine))
+    cot_theirs = jnp.concatenate(cot_of(theirs))
+    cot_before = jnp.where(lower, low[2 * WAVES - 1], low[WAVES - 1])
+    cot_after = jnp.where(lower, high[WAVES - 2], high[2 * WAVES - 2])
     cot_around = jnp.concatenate(
-        [low[-1], cot_chip.reshape(CHIP, 128), high[-1]], axis=0
+        [
+            cot_before,
+            jnp.where(lower, cot_mine, cot_theirs),
+            jnp.where(lower, cot_theirs, cot_mine),
+            cot_after,
+        ]
     )
     cot_rows = jnp.pad(lax.dynamic_slice_in_dim(cot_around, 32 * core + 5, 38, 0), ((0, 2), (0, 0)))
     right_edge = cot_rows[1:37, 126:128].T
@@ -573,12 +599,8 @@
         + jnp.where((same_core & (target_cell == cell - 1))[:, None, None], to_left[None], 0.0)
     )
 
-    velocity_all = jnp.concatenate(
-        [low[2 * CHIP + CHIP - 8 : 3 * CHIP], velocity_chip, high[2 * CHIP : 2 * CHIP + 8]], axis=0
-    )
-    velocity_rows = lax.dynamic_slice_in_dim(velocity_all, 32 * core + 5, 38, 0).reshape(38, 1024)
     velocity_wide = lax.dynamic_slice_in_dim(
-        jnp.pad(velocity_rows, ((0, 2), (3, 253))), 128 * cell, 256, 1
+        jnp.pad(velocity_rows.reshape(40, 1024), ((0, 0), (3, 253))), 128 * cell, 256, 1
     )
     velocity_wide = jnp.where(jnp.arange(256)[None, :] < 134, velocity_wide, 0.0)
 
@@ -616,9 +638,10 @@
 
     pieces = call(
         adjoint_kernel,
-        [vmem()] * 8,
+        [smem()] + [vmem()] * 8,
         f32(16, 48, 128),
-        [scratch(2, WIDE, 8, 128), scratch(CHIP * 8, 128), scratch(8, 128, 128)],
+        [scratch(2, WIDE, 8, 128), scratch(CHIP, 8, 128), scratch(8, 128, 128)],
+        core_id,
         counts,
         recorded,
         low_adjoint,
@@ -638,7 +661,7 @@
     new_velocity, grads = call(
         network_kernel,
         [smem()] + [vmem()] * 10,
-        (f32(32, 128), f32(CH, 512)),
+        (f32(32, 128), f32(CH, 384)),
         [
             scratch(8, FLAT + 2 * SIDE),
             scratch(160, FLAT, dtype=bf16),
@@ -655,7 +678,7 @@
             scratch(128, FLAT, dtype=bf16),
             scratch(8, FLAT),
         ],
-        core.reshape(1).astype(jnp.int32),
+        core_id,
         summed,
         arrived,
         velocity_wide,
@@ -673,7 +696,7 @@
     total = over_fours(total, "band_1", [(0, 2, 4, 6), (1, 3, 5, 7)])
     total = over_pairs(total, "band_1", [(0, 1), (2, 3), (4, 5), (6, 7)])
     grad_mid = total[:, 0:288]
-    outer = total[:, 384:456].reshape(CH, 9, 8)
+    outer = total[:, 288:360].reshape(CH, 9, 8)
     grad_in = outer[:, :, 0:2].reshape(CH, 18)
     grad_out = outer[:, ::-1, 2].T.reshape(1, 9 * CH)
     return new_velocity, grad_in, grad_mid, grad_out

time: 215 us -> 158 us (0.73)
  Pallas kernels: 101 us -> 57 us
  waiting for transfers between devices: 43 us -> 29 us
    pallas_call x3 -> x4, Pallas kernels: 101 us -> 57 us  [call(): pl.pallas_call(kernel, in_specs=in_specs, out_specs=tuple((vmem() for _ i...]
    ppermute x3, waiting for transfers between devices: 12.2 us -> 0.78 us  [the longest x1 0.78 us: on_device(): lax.ppermute(given.reshape(packed_rows, 8, 128), CORE, [(0, 1), (1, 0)])]
    unnamed x59 -> x43, local copies, waits for them, and re-layouts: 7.02 us -> 1.84 us
    ppermute x9, starting transfers between devices: 21 us -> 18 us  [over_fours(): lax.ppermute(x, axis, [(group[i], group[i ^ turn]) for group in groups fo...]
    slice x11 -> x6, local copies, waits for them, and re-layouts: 0.83 us -> 3.15 us  [the longest x2 1.05 us: on_device(): waves = jnp.concatenate([mine[:WAVES], theirs[:WAVES]])]
  transfers between devices with their start and end apart: 18 -> 18, of which waited for: 13 -> 11; matrix products, arithmetic and copies ran while one was open for 7% -> 14% of each run, Pallas kernels for 21% -> 14%
where the time goes in v2:
time: 158 us; the launch traced here: 156 us
  Pallas kernels  57 us (36%)
  starting transfers between devices  40.7 us (26%)
  waiting for transfers between devices  29 us (18%)
  local copies, waits for them, and re-layouts  16 us (10%)
  other arithmetic  10.1 us (6%)
  between operations  2.94 us (2%)
    pallas_call x4, Pallas kernels, call(): pl.pallas_call(kernel, in_specs=in_specs, out_specs=tuple((vmem() for _ i...  57 us
    ppermute x9, starting transfers between devices, over_fours(): lax.ppermute(x, axis, [(group[i], group[i ^ turn]) for group in groups fo...  18 us
    ppermute x9, waiting for transfers between devices, over_fours(): lax.ppermute(x, axis, [(group[i], group[i ^ turn]) for group in groups fo...  12.4 us
    all_to_all x1, waiting for transfers between devices, on_device(): summed = jnp.sum(lax.all_to_all(pieces, SUMMED, 0, 0, tiled=True), axis=0)  9.45 us
    all_to_all x1, starting transfers between devices, on_device(): summed = jnp.sum(lax.all_to_all(pieces, SUMMED, 0, 0, tiled=True), axis=0)  7.03 us
    ppermute x2, waiting for transfers between devices, over_pairs(): lax.ppermute(x, axis, [(a, b) for a, b in groups] + [(b, a) for a, b in g...  4.65 us
    ppermute x1, starting transfers between devices, on_device(): low = lax.ppermute(waves, CHIPS, up)  3.83 us
    ppermute x1, starting transfers between devices, on_device(): low_adjoint = lax.ppermute(adjoints, CHIPS, up)  3.78 us
  transfers between devices with their start and end apart: 18, of which 11 were waited for; matrix products, arithmetic and copies ran while one was open for 14% of the time, Pallas kernels for 14%

profile of v2, /device:TPU:32, one launch (start us, length us, event | category | flops | bytes accessed | tf_op | source)
XLA Modules:
  0.0 156.3 jit_solution(17075803463336226871)
XLA Ops:
  0.7 2.5 %shard_map.210 = (f32[1312,128]{1,0:T(8,128)}, f32[1312,128]{1,0:T(8,128)}) custom-call(s32[1]{0:T(128)} %bitcast.core_ref.core, f32[2,32,1024]{2,1,0:T(8,128)} %now.1, f32[2,32,1024]{2,1,0:T(8,128)} %before.1, f32[2,32,1024]{2,1,0:T(8,128)} %last.1, f32[2,32,1024]{2,1,0:T(8,128)} %after.1, f32[32,1024]{1,0:T(8,128)} %velocity.1, f32[32,128]{1,0:T(8,128)} %cotangent.1), custom_call_target="tpu_custom_call" | custom-call | tf_op jit(solution)/shard_map/pallas_call | solution.py:452
  3.8 1.0 slice_bitcast_fusion
  6.5 3.8 %collective-permute-start.3 = (f32[196,8,128]{2,1,0:T(8,128)S(1)}, f32[196,8,128]{2,1,0:T(8,128)S(1)}, u32[]{:S(2)}, u32[]{:S(2)}) collective-permute-start(f32[196,8,128]{2,1,0:T(8,128)S(1)} %pad_maximum_fusion.mid), channel_id=1, source_target_pairs={{0,4},{4,8},{8,12},{12,16},{16,20},{20,24},{24,28},{28,32},{32,36}... | collective-permute-start | bytes 2408456 | tf_op jit(solution)/shard_map/ppermute | solution.py:526
  10.4 2.1 %collective-permute-start.4 = (f32[196,8,128]{2,1,0:T(8,128)S(1)}, f32[196,8,128]{2,1,0:T(8,128)S(1)}, u32[]{:S(2)}, u32[]{:S(2)}) collective-permute-start(f32[196,8,128]{2,1,0:T(8,128)S(1)} %pad_maximum_fusion.mid), channel_id=1, source_target_pairs={{4,0},{8,4},{12,8},{16,12},{20,16},{24,20},{28,24},{32,28},{36,32}... | collective-permute-start | bytes 2408456 | tf_op jit(solution)/shard_map/ppermute | solution.py:527
  12.4 1.0 slice.80
  13.4 1.0 slice.81
  14.4 1.3 slice_bitcast_fusion.6
  19.4 1.2 compare_select_fusion.source
  24.1 3.8 %collective-permute-start.1 = (f32[128,8,128]{2,1,0:T(8,128)S(1)}, f32[128,8,128]{2,1,0:T(8,128)}, u32[]{:S(2)}, u32[]{:S(2)}) collective-permute-start(f32[128,8,128]{2,1,0:T(8,128)S(1)} %pad_maximum_fusion.1.mid), channel_id=1, source_target_pairs={{0,4},{4,8},{8,12},{12,16},{16,20},{20,24},{24,28},{28,32},{32,36}... | collective-permute-start | bytes 1572872 | tf_op jit(solution)/shard_map/ppermute | solution.py:558
  27.9 3.1 %collective-permute-start.2 = (f32[128,8,128]{2,1,0:T(8,128)S(1)}, f32[128,8,128]{2,1,0:T(8,128)}, u32[]{:S(2)}, u32[]{:S(2)}) collective-permute-start(f32[128,8,128]{2,1,0:T(8,128)S(1)} %pad_maximum_fusion.1.mid), channel_id=1, source_target_pairs={{4,0},{8,4},{12,8},{16,12},{20,16},{24,20},{28,24},{32,28},{36,32}... | collective-permute-start | bytes 1572872 | tf_op jit(solution)/shard_map/ppermute | solution.py:559
  34.5 1.2 fusion.35.pulses
  38.2 22.7 %shard_map.211 = (f32[16,64,8,128]{3,2,1,0:T(8,128)}, f32[192,8,128]{2,1,0:T(8,128)}, f32[40,8,128]{2,1,0:T(8,128)}) custom-call(s32[1]{0:T(128)} %bitcast.core_ref.core, f32[16]{0:T(128)} %fusion.35.pulses, f32[8,128]{1,0:T(8,128)} %compare_select_fusion.source, f32[196,8,128]{2,1,0:T(8,128)} %copy-done.3, f32[196,8,128]{2,1,0:T(8,128)} %copy-done.1, ...), custom_call_target="tpu_custom_call" | custom-call | tf_op jit(solution)/shard_map/pallas_call | solution.py:452
  61.7 22.8 %shard_map.212 = f32[16,48,128]{2,1,0:T(8,128)} custom-call(s32[1]{0:T(128)} %bitcast.core_ref.core, f32[8,128]{1,0:T(8,128)} %bitcast.84, f32[16,8,128]{2,1,0:T(8,128)} %copy.42.recorded, f32[128,8,128]{2,1,0:T(8,128)} %collective-permute-done.1.low, f32[128,8,128]{2,1,0:T(8,128)} %copy-done.2, f32[128,8,128]{2,1,0:T(8,128)} %collective-permute-done.2.high, ...), custom_call_target="tpu_custom_call" | custom-call | tf_op jit(solution)/shard_map/pallas_call | solution.py:452
  84.5 7.0 %all-to-all-start = ((f32[16,48,128]{2,1,0:T(8,128)}), f32[16,48,128]{2,1,0:T(8,128)S(1)}, u32[]{:S(2)}, u32[]{:S(2)}) async-start(f32[16,48,128]{2,1,0:T(8,128)} %shard_map.212), calls=%async_computation | async-start | bytes 786432 | tf_op jit(solution)/shard_map/all_to_all | solution.py:654
  93.1 9.5 %all-to-all-done = f32[16,48,128]{2,1,0:T(8,128)S(1)} async-done(((f32[16,48,128]{2,1,0:T(8,128)}), f32[16,48,128]{2,1,0:T(8,128)S(1)}, u32[]{:S(2)}, u32[]{:S(2)}) %all-to-all-start) | async-done | bytes 393248 | tf_op jit(solution)/shard_map/all_to_all | solution.py:654
  102.6 1.9 %collective-permute-start.5 = (f32[16,128]{1,0:T(8,128)S(1)}, f32[16,128]{1,0:T(8,128)S(1)}, u32[]{:S(2)}, u32[]{:S(2)}) collective-permute-start(f32[16,128]{1,0:T(8,128)S(1)} %pad_maximum_fusion.7), channel_id=1, source_target_pairs={{4,2},{8,6},{12,10},{16,14},{20,18},{24,22},{28,26},{32,30},{36,34... | collective-permute-start | bytes 24584 | tf_op jit(solution)/shard_map/ppermute | solution.py:658
  105.9 1.7 %collective-permute-done.5.arrived = f32[16,128]{1,0:T(8,128)S(1)} collective-permute-done((f32[16,128]{1,0:T(8,128)S(1)}, f32[16,128]{1,0:T(8,128)S(1)}, u32[]{:S(2)}, u32[]{:S(2)}) %collective-permute-start.5) | collective-permute-done | bytes 8224 | tf_op jit(solution)/shard_map/ppermute | solution.py:658
  109.0 9.0 %shard_map.213 = (f32[32,128]{1,0:T(8,128)}, f32[32,384]{1,0:T(8,128)}) custom-call(s32[1]{0:T(128)} %bitcast.core_ref.core, f32[48,128]{1,0:T(8,128)} %copy-done.7, f32[16,128]{1,0:T(8,128)} %copy-done.12, f32[40,256]{1,0:T(8,128)} %fusion.14.velocity_wide, f32[40,128]{1,0:T(8,128)} %pad.32.cotangent_rows, f32[8,5376]{1,0:T(8,128)} %broadcast_in_dim.65.inside, ...), custom_call_target="tpu_custom_call" | custom-call | tf_op jit(solution)/shard_map/pallas_call | solution.py:452
  118.4 1.1 collective-permute-done.6
  120.3 2.2 %collective-permute-start.8 = (f32[32,384]{1,0:T(8,128)S(1)}, f32[32,384]{1,0:T(8,128)S(1)}, u32[]{:S(2)}, u32[]{:S(2)}) collective-permute-start(f32[32,384]{1,0:T(8,128)S(1)} %add.194), channel_id=1, source_target_pairs={{0,128},{64,192},{128,0},{192,64},{1,129},{65,193},{129,1},{193,65... | collective-permute-start | bytes 147464 | tf_op jit(solution)/shard_map/ppermute | solution.py:479
  122.5 2.5 %collective-permute-start.9 = (f32[32,384]{1,0:T(8,128)S(1)}, f32[32,384]{1,0:T(8,128)S(1)}, u32[]{:S(2)}, u32[]{:S(2)}) collective-permute-start(f32[32,384]{1,0:T(8,128)S(1)} %add.194), channel_id=1, source_target_pairs={{0,192},{64,128},{128,64},{192,0},{1,193},{65,129},{129,65},{193,1... | collective-permute-start | bytes 147464 | tf_op jit(solution)/shard_map/ppermute | solution.py:479
  125.0 1.0 collective-permute-done.8
  126.0 1.8 %collective-permute-done.9 = f32[32,384]{1,0:T(8,128)S(1)} collective-permute-done((f32[32,384]{1,0:T(8,128)S(1)}, f32[32,384]{1,0:T(8,128)S(1)}, u32[]{:S(2)}, u32[]{:S(2)}) %collective-permute-start.9) | collective-permute-done | bytes 49184 | tf_op jit(solution)/shard_map/ppermute | solution.py:479
  128.3 3.9 %collective-permute-start.11 = (f32[32,384]{1,0:T(8,128)S(1)}, f32[32,384]{1,0:T(8,128)S(1)}, u32[]{:S(2)}, u32[]{:S(2)}) collective-permute-start(f32[32,384]{1,0:T(8,128)S(1)} %add_add_fusion.2), channel_id=1, source_target_pairs={{0,32},{1,33},{32,0},{33,1},{2,34},{3,35},{34,2},{35,3},{4,36},{5,... | collective-permute-start | bytes 147464 | tf_op jit(solution)/shard_map/ppermute | solution.py:479
  132.2 2.3 %collective-permute-start.12 = (f32[32,384]{1,0:T(8,128)S(1)}, f32[32,384]{1,0:T(8,128)S(1)}, u32[]{:S(2)}, u32[]{:S(2)}) collective-permute-start(f32[32,384]{1,0:T(8,128)S(1)} %add_add_fusion.2), channel_id=1, source_target_pairs={{0,33},{1,32},{32,1},{33,0},{2,35},{3,34},{34,3},{35,2},{4,37},{5,... | collective-permute-start | bytes 147464 | tf_op jit(solution)/shard_map/ppermute | solution.py:479
  134.8 2.7 %collective-permute-done.12 = f32[32,384]{1,0:T(8,128)S(1)} collective-permute-done((f32[32,384]{1,0:T(8,128)S(1)}, f32[32,384]{1,0:T(8,128)S(1)}, u32[]{:S(2)}, u32[]{:S(2)}) %collective-permute-start.12) | collective-permute-done | bytes 49184 | tf_op jit(solution)/shard_map/ppermute | solution.py:479
  137.5 2.7 %collective-permute-start.13 = (f32[32,384]{1,0:T(8,128)S(1)}, f32[32,384]{1,0:T(8,128)S(1)}, u32[]{:S(2)}, u32[]{:S(2)}) collective-permute-start(f32[32,384]{1,0:T(8,128)S(1)} %add_add_fusion.1), channel_id=1, source_target_pairs={{0,8},{8,0},{16,24},{24,16},{4,12},{12,4},{20,28},{28,20},{1,9},{9... | collective-permute-start | bytes 147464 | tf_op jit(solution)/shard_map/ppermute | solution.py:479
  140.2 2.7 %collective-permute-start.14 = (f32[32,384]{1,0:T(8,128)S(1)}, f32[32,384]{1,0:T(8,128)S(1)}, u32[]{:S(2)}, u32[]{:S(2)}) collective-permute-start(f32[32,384]{1,0:T(8,128)S(1)} %add_add_fusion.1), channel_id=1, source_target_pairs={{0,16},{8,24},{16,0},{24,8},{4,20},{12,28},{20,4},{28,12},{1,17},{... | collective-permute-start | bytes 147464 | tf_op jit(solution)/shard_map/ppermute | solution.py:479
  142.9 1.2 collective-permute-start.15
  144.1 4.6 %collective-permute-done.14 = f32[32,384]{1,0:T(8,128)S(1)} collective-permute-done((f32[32,384]{1,0:T(8,128)S(1)}, f32[32,384]{1,0:T(8,128)S(1)}, u32[]{:S(2)}, u32[]{:S(2)}) %collective-permute-start.14) | collective-permute-done | bytes 49184 | tf_op jit(solution)/shard_map/ppermute | solution.py:479
  148.7 2.0 %collective-permute-done.15 = f32[32,384]{1,0:T(8,128)S(1)} collective-permute-done((f32[32,384]{1,0:T(8,128)S(1)}, f32[32,384]{1,0:T(8,128)S(1)}, u32[]{:S(2)}, u32[]{:S(2)}) %collective-permute-start.15) | collective-permute-done | bytes 49184 | tf_op jit(solution)/shard_map/ppermute | solution.py:479
  151.3 3.6 %collective-permute-done.16 = f32[32,384]{1,0:T(8,128)S(1)} collective-permute-done((f32[32,384]{1,0:T(8,128)S(1)}, f32[32,384]{1,0:T(8,128)S(1)}, u32[]{:S(2)}, u32[]{:S(2)}) %collective-permute-start.16) | collective-permute-done | bytes 49184 | tf_op jit(solution)/shard_map/ppermute | solution.py:474
  (121 shorter events, 22.6 us)
Async XLA Ops:
  0.6 22.7 %copy-start = (f32[2,16,128]{2,1,0:T(8,128)S(1)}, f32[2,16,128]{2,1,0:T(8,128)}, u32[]{:S(2)}) copy-start(f32[2,16,128]{2,1,0:T(8,128)} %param.29) | copy-start | bytes 49156
  0.7 15.1 %copy-start.15 = (s32[2]{0:T(128)S(1)}, s32[2]{0:T(128)}, u32[]{:S(2)}) copy-start(s32[2]{0:T(128)} %param.25) | copy-start | bytes 28
  0.7 15.7 %copy-start.16 = (s32[2]{0:T(128)S(1)}, s32[2]{0:T(128)}, u32[]{:S(2)}) copy-start(s32[2]{0:T(128)} %param.26) | copy-start | bytes 28
  0.7 16.2 %copy-start.17 = (s32[2]{0:T(128)S(1)}, s32[2]{0:T(128)}, u32[]{:S(2)}) copy-start(s32[2]{0:T(128)} %param.27) | copy-start | bytes 28
  0.7 16.9 %copy-start.18 = (s32[2]{0:T(128)S(1)}, s32[2]{0:T(128)}, u32[]{:S(2)}) copy-start(s32[2]{0:T(128)} %param.28) | copy-start | bytes 28
  3.2 2.3 %collective-permute-start = (f32[164,8,128]{2,1,0:T(8,128)}, f32[164,8,128]{2,1,0:T(8,128)S(1)}, u32[]{:S(2)}, u32[]{:S(2)}) collective-permute-start(f32[164,8,128]{2,1,0:T(8,128)} %bitcast.85), channel_id=1, source_target_pairs={{0,2},{2,0},{1,3},{3,1},{4,6},{6,4},{5,7},{7,5},{8,10},{10,8},{9,1... | collective-permute-start | bytes 2015240 | tf_op jit(solution)/shard_map/ppermute | solution.py:522
  6.5 31.0 %copy-start.1 = (f32[196,8,128]{2,1,0:T(8,128)}, f32[196,8,128]{2,1,0:T(8,128)S(1)}, u32[]{:S(2)}) copy-start(f32[196,8,128]{2,1,0:T(8,128)S(1)} %pad_maximum_fusion.mid) | copy-start | bytes 2408452
  6.5 30.6 %collective-permute-start.3 = (f32[196,8,128]{2,1,0:T(8,128)S(1)}, f32[196,8,128]{2,1,0:T(8,128)S(1)}, u32[]{:S(2)}, u32[]{:S(2)}) collective-permute-start(f32[196,8,128]{2,1,0:T(8,128)S(1)} %pad_maximum_fusion.mid), channel_id=1, source_target_pairs={{0,4},{4,8},{8,12},{12,16},{16,20},{20,24},{24,28},{28,32},{32,36}... | collective-permute-start | bytes 2408456 | tf_op jit(solution)/shard_map/ppermute | solution.py:526
  10.4 26.7 %collective-permute-start.4 = (f32[196,8,128]{2,1,0:T(8,128)S(1)}, f32[196,8,128]{2,1,0:T(8,128)S(1)}, u32[]{:S(2)}, u32[]{:S(2)}) collective-permute-start(f32[196,8,128]{2,1,0:T(8,128)S(1)} %pad_maximum_fusion.mid), channel_id=1, source_target_pairs={{4,0},{8,4},{12,8},{16,12},{20,16},{24,20},{28,24},{32,28},{36,32}... | collective-permute-start | bytes 2408456 | tf_op jit(solution)/shard_map/ppermute | solution.py:527
  24.1 37.6 %copy-start.2 = (f32[128,8,128]{2,1,0:T(8,128)}, f32[128,8,128]{2,1,0:T(8,128)S(1)}, u32[]{:S(2)}) copy-start(f32[128,8,128]{2,1,0:T(8,128)S(1)} %pad_maximum_fusion.1.mid) | copy-start | bytes 1572868
  24.1 37.6 %collective-permute-start.1 = (f32[128,8,128]{2,1,0:T(8,128)S(1)}, f32[128,8,128]{2,1,0:T(8,128)}, u32[]{:S(2)}, u32[]{:S(2)}) collective-permute-start(f32[128,8,128]{2,1,0:T(8,128)S(1)} %pad_maximum_fusion.1.mid), channel_id=1, source_target_pairs={{0,4},{4,8},{8,12},{12,16},{16,20},{20,24},{24,28},{28,32},{32,36}... | collective-permute-start | bytes 1572872 | tf_op jit(solution)/shard_map/ppermute | solution.py:558
  27.9 33.8 %collective-permute-start.2 = (f32[128,8,128]{2,1,0:T(8,128)S(1)}, f32[128,8,128]{2,1,0:T(8,128)}, u32[]{:S(2)}, u32[]{:S(2)}) collective-permute-start(f32[128,8,128]{2,1,0:T(8,128)S(1)} %pad_maximum_fusion.1.mid), channel_id=1, source_target_pairs={{4,0},{8,4},{12,8},{16,12},{20,16},{24,20},{28,24},{32,28},{36,32}... | collective-permute-start | bytes 1572872 | tf_op jit(solution)/shard_map/ppermute | solution.py:559
  60.9 32.1 %copy-start.10 = (s32[5376]{0:T(1024)S(1)}, s32[5376]{0:T(1024)}, u32[]{:S(2)}) copy-start(s32[5376]{0:T(1024)} %constant.141.clone) | copy-start | bytes 64516
  60.9 32.1 %copy-start.11 = (s32[5376]{0:T(1024)S(1)}, s32[5376]{0:T(1024)}, u32[]{:S(2)}) copy-start(s32[5376]{0:T(1024)} %constant.142.clone) | copy-start | bytes 64516
  60.9 32.1 %copy-start.13 = (pred[5376]{0:T(1024)(128)(4,1)S(1)}, pred[5376]{0:T(1024)(128)(4,1)}, u32[]{:S(2)}) copy-start(pred[5376]{0:T(1024)(128)(4,1)} %constant.143.clone) | copy-start | bytes 16132
  61.7 31.4 %copy-start.6 = (f32[40,8,128]{2,1,0:T(8,128)S(1)}, f32[40,8,128]{2,1,0:T(8,128)}, u32[]{:S(2)}) copy-start(f32[40,8,128]{2,1,0:T(8,128)} %get-tuple-element.48) | copy-start | bytes 491524
  61.7 42.9 %copy-start.14 = (pred[256]{0:T(512)(128)(4,1)S(1)}, pred[256]{0:T(512)(128)(4,1)}, u32[]{:S(2)}) copy-start(pred[256]{0:T(512)(128)(4,1)} %iota_compare_fusion.2) | copy-start | bytes 772
  61.7 46.6 %copy-start.9 = (f32[5376]{0:T(1024)S(1)}, f32[5376]{0:T(1024)}, u32[]{:S(2)}) copy-start(f32[5376]{0:T(1024)} %constant.140.clone) | copy-start | bytes 64516
  84.5 18.1 %all-to-all-start = ((f32[16,48,128]{2,1,0:T(8,128)}), f32[16,48,128]{2,1,0:T(8,128)S(1)}, u32[]{:S(2)}, u32[]{:S(2)}) async-start(f32[16,48,128]{2,1,0:T(8,128)} %shard_map.212), calls=%async_computation | async-start | bytes 786432 | tf_op jit(solution)/shard_map/all_to_all | solution.py:654
  102.6 6.4 %copy-start.7 = (f32[48,128]{1,0:T(8,128)}, f32[48,128]{1,0:T(8,128)S(1)}, u32[]{:S(2)}) copy-start(f32[48,128]{1,0:T(8,128)S(1)} %reduce_sum.19.summed) | copy-start | bytes 73732
  102.6 5.0 %collective-permute-start.5 = (f32[16,128]{1,0:T(8,128)S(1)}, f32[16,128]{1,0:T(8,128)S(1)}, u32[]{:S(2)}, u32[]{:S(2)}) collective-permute-start(f32[16,128]{1,0:T(8,128)S(1)} %pad_maximum_fusion.7), channel_id=1, source_target_pairs={{4,2},{8,6},{12,10},{16,14},{20,18},{24,22},{28,26},{32,30},{36,34... | collective-permute-start | bytes 24584 | tf_op jit(solution)/shard_map/ppermute | solution.py:658
  117.9 1.5 collective-permute-start.6
  120.3 4.7 %collective-permute-start.7 = (f32[32,384]{1,0:T(8,128)S(1)}, f32[32,384]{1,0:T(8,128)S(1)}, u32[]{:S(2)}, u32[]{:S(2)}) collective-permute-start(f32[32,384]{1,0:T(8,128)S(1)} %add.194), channel_id=1, source_target_pairs={{0,64},{64,0},{128,192},{192,128},{1,65},{65,1},{129,193},{193,129... | collective-permute-start | bytes 147464 | tf_op jit(solution)/shard_map/ppermute | solution.py:479
  120.3 5.7 %collective-permute-start.8 = (f32[32,384]{1,0:T(8,128)S(1)}, f32[32,384]{1,0:T(8,128)S(1)}, u32[]{:S(2)}, u32[]{:S(2)}) collective-permute-start(f32[32,384]{1,0:T(8,128)S(1)} %add.194), channel_id=1, source_target_pairs={{0,128},{64,192},{128,0},{192,64},{1,129},{65,193},{129,1},{193,65... | collective-permute-start | bytes 147464 | tf_op jit(solution)/shard_map/ppermute | solution.py:479
  122.5 5.3 %collective-permute-start.9 = (f32[32,384]{1,0:T(8,128)S(1)}, f32[32,384]{1,0:T(8,128)S(1)}, u32[]{:S(2)}, u32[]{:S(2)}) collective-permute-start(f32[32,384]{1,0:T(8,128)S(1)} %add.194), channel_id=1, source_target_pairs={{0,192},{64,128},{128,64},{192,0},{1,193},{65,129},{129,65},{193,1... | collective-permute-start | bytes 147464 | tf_op jit(solution)/shard_map/ppermute | solution.py:479
  127.8 6.7 %collective-permute-start.10 = (f32[32,384]{1,0:T(8,128)S(1)}, f32[32,384]{1,0:T(8,128)S(1)}, u32[]{:S(2)}, u32[]{:S(2)}) collective-permute-start(f32[32,384]{1,0:T(8,128)S(1)} %add_add_fusion.2), channel_id=1, source_target_pairs={{0,1},{1,0},{32,33},{33,32},{2,3},{3,2},{34,35},{35,34},{4,5},{5,4... | collective-permute-start | bytes 147464 | tf_op jit(solution)/shard_map/ppermute | solution.py:479
  128.3 6.5 %collective-permute-start.11 = (f32[32,384]{1,0:T(8,128)S(1)}, f32[32,384]{1,0:T(8,128)S(1)}, u32[]{:S(2)}, u32[]{:S(2)}) collective-permute-start(f32[32,384]{1,0:T(8,128)S(1)} %add_add_fusion.2), channel_id=1, source_target_pairs={{0,32},{1,33},{32,0},{33,1},{2,34},{3,35},{34,2},{35,3},{4,36},{5,... | collective-permute-start | bytes 147464 | tf_op jit(solution)/shard_map/ppermute | solution.py:479
  132.2 5.3 %collective-permute-start.12 = (f32[32,384]{1,0:T(8,128)S(1)}, f32[32,384]{1,0:T(8,128)S(1)}, u32[]{:S(2)}, u32[]{:S(2)}) collective-permute-start(f32[32,384]{1,0:T(8,128)S(1)} %add_add_fusion.2), channel_id=1, source_target_pairs={{0,33},{1,32},{32,1},{33,0},{2,35},{3,34},{34,3},{35,2},{4,37},{5,... | collective-permute-start | bytes 147464 | tf_op jit(solution)/shard_map/ppermute | solution.py:479
  137.5 6.6 %collective-permute-start.13 = (f32[32,384]{1,0:T(8,128)S(1)}, f32[32,384]{1,0:T(8,128)S(1)}, u32[]{:S(2)}, u32[]{:S(2)}) collective-permute-start(f32[32,384]{1,0:T(8,128)S(1)} %add_add_fusion.1), channel_id=1, source_target_pairs={{0,8},{8,0},{16,24},{24,16},{4,12},{12,4},{20,28},{28,20},{1,9},{9... | collective-permute-start | bytes 147464 | tf_op jit(solution)/shard_map/ppermute | solution.py:479
  140.2 8.5 %collective-permute-start.14 = (f32[32,384]{1,0:T(8,128)S(1)}, f32[32,384]{1,0:T(8,128)S(1)}, u32[]{:S(2)}, u32[]{:S(2)}) collective-permute-start(f32[32,384]{1,0:T(8,128)S(1)} %add_add_fusion.1), channel_id=1, source_target_pairs={{0,16},{8,24},{16,0},{24,8},{4,20},{12,28},{20,4},{28,12},{1,17},{... | collective-permute-start | bytes 147464 | tf_op jit(solution)/shard_map/ppermute | solution.py:479
  142.9 7.8 %collective-permute-start.15 = (f32[32,384]{1,0:T(8,128)S(1)}, f32[32,384]{1,0:T(8,128)S(1)}, u32[]{:S(2)}, u32[]{:S(2)}) collective-permute-start(f32[32,384]{1,0:T(8,128)S(1)} %add_add_fusion.1), channel_id=1, source_target_pairs={{0,24},{8,16},{16,8},{24,0},{4,28},{12,20},{20,12},{28,4},{1,25},{... | collective-permute-start | bytes 147464 | tf_op jit(solution)/shard_map/ppermute | solution.py:479
  150.7 4.2 %collective-permute-start.16 = (f32[32,384]{1,0:T(8,128)S(1)}, f32[32,384]{1,0:T(8,128)S(1)}, u32[]{:S(2)}, u32[]{:S(2)}) collective-permute-start(f32[32,384]{1,0:T(8,128)S(1)} %add_add_fusion), channel_id=1, source_target_pairs={{0,4},{8,12},{16,20},{24,28},{4,0},{12,8},{20,16},{28,24},{1,5},{9... | collective-permute-start | bytes 147464 | tf_op jit(solution)/shard_map/ppermute | solution.py:474
  (5 other events, 5.7 us)
